TPU v7x, 32 devices: a whole 2x2x4 slice. The times are simulated.
32 devices in a mesh: row: 4 (over z), col: 8 (over y, x, core).
Axes of the slice: x: 2, y: 2, z: 4, core: 2. Of those that a mesh axis runs over, the one named last changes fastest.
Arguments:
- inv_depth: float32 [64, 3072], P(('row', 'col')), may hold values from 0.2 to 1
- rotation: float32 [3, 64], P(None, ('row', 'col')), may hold values from -0.05 to 0.05
- translation: float32 [3, 64], P(None, ('row', 'col')), may hold values from -0.25 to 0.25
- edge_target: int32 [64, 24], P(('row', 'col')), may hold values from 0 to 63, as said below
- flow_obs: float32 [2, 64, 24, 3072], P(None, ('row', 'col')), may hold values from -2.8 to 2.8
- weight: float32 [2, 64, 24, 3072], P(None, ('row', 'col')), may hold values from 0.1 to 1
Outputs:
- depth_next: float32 [64, 3072], P(('row', 'col'))
- pose_step: float32 [6, 64], P(None, ('row', 'col'))
Inputs may be any that keep to these rules, and one draw needn't show every extreme that they name: `edge_target`: each keyframe's targets are distinct, differ from the keyframe itself, are sorted ascending, and lie in the keyframe's own block of 16 consecutive keyframes or in one of the two neighbouring blocks, the blocks counted cyclically.
All inputs are finite; a program needn't handle non-finite values.
Results may differ from a plain program's by a relative error of at most 0.0003.
Values sent between devices are 32-bit elements; how exact they have to be, the bound alone decides.
No kernel may reach another device: no remote copies, remote signals or barrier semaphores. Data moves between devices by JAX's collectives and lax.ppermute only.
A program may use at most 128 MiB of HBM per device.

v0:
```python
import jax
import jax.numpy as jnp
from jax import lax
from jax.sharding import PartitionSpec as P

IMG_H = 48
IMG_W = 64


PRECISE = lax.Precision.HIGHEST
DAMP_DEPTH = 0.1
LEVENBERG = 0.1
RIDGE = 0.001


def with_halo(cells, sides, width):
    for axis, dim in sides:
        count = lax.axis_size(axis)
        head = lax.slice_in_dim(cells, 0, width, axis=dim)
        tail = lax.slice_in_dim(cells, cells.shape[dim] - width, cells.shape[dim], axis=dim)
        cells = jnp.concatenate(
            [
                lax.ppermute(tail, axis, [(i, (i + 1) % count) for i in range(count)]),
                cells,
                lax.ppermute(head, axis, [((i + 1) % count, i) for i in range(count)]),
            ],
            axis=dim,
        )
    return cells


def from_behind(shard, axis, by):
    devices = lax.axis_size(axis)
    return lax.ppermute(shard, axis, [(i, (i + by) % devices) for i in range(devices)])


def pixel_grid(pixel_count):
    pixel_index = jnp.arange(pixel_count, dtype=jnp.int32)
    across = (pixel_index % IMG_W).astype(jnp.float32)
    downward = (pixel_index // IMG_W).astype(jnp.float32)
    return ((across + 0.5) / IMG_W - 0.5, (downward + 0.5 - 0.5 * IMG_H) / IMG_W)


def edge_terms(relative, target_depth, flows, weights, across, downward):
    spin_x, spin_y, spin_z, move_x, move_y, move_z = [relative[i][:, None] for i in range(6)]
    point_x = across + spin_y - spin_z * downward + move_x * target_depth
    point_y = downward + spin_z * across - spin_x + move_y * target_depth
    point_z = 1.0 + spin_x * downward - spin_y * across + move_z * target_depth
    recip_z = 1.0 / point_z
    image_u = point_x * recip_z
    image_v = point_y * recip_z
    resid_u = flows[0] - (image_u - across)
    resid_v = flows[1] - (image_v - downward)
    slope_u = recip_z * (move_x - image_u * move_z)
    slope_v = recip_z * (move_y - image_v * move_z)
    depth_recip = target_depth * recip_z
    blank_map = jnp.zeros_like(recip_z)
    jac_u = jnp.stack(
        [
            -image_u * downward * recip_z,
            (1.0 + image_u * across) * recip_z,
            -downward * recip_z,
            depth_recip,
            blank_map,
            -image_u * depth_recip,
        ]
    )
    jac_v = jnp.stack(
        [
            (-1.0 - image_v * downward) * recip_z,
            image_v * across * recip_z,
            across * recip_z,
            blank_map,
            depth_recip,
            -image_v * depth_recip,
        ]
    )
    weight_u = weights[0]
    weight_v = weights[1]
    depth_grad = weight_u * slope_u * resid_u + weight_v * slope_v * resid_v
    depth_curv = weight_u * slope_u * slope_u + weight_v * slope_v * slope_v
    scaled_u = weight_u * jac_u
    scaled_v = weight_v * jac_v
    coupling = scaled_u * slope_u + scaled_v * slope_v
    block = jnp.einsum("aep,bep->eab", scaled_u, jac_u, precision=PRECISE) + jnp.einsum(
        "aep,bep->eab", scaled_v, jac_v, precision=PRECISE
    )
    pose_grad = jnp.einsum("aep,ep->ea", scaled_u, resid_u, precision=PRECISE) + jnp.einsum(
        "aep,ep->ea", scaled_v, resid_v, precision=PRECISE
    )
    return (depth_grad, depth_curv, coupling, block, pose_grad)


def solve_frames(block_table):
    frame_count = block_table.shape[0]
    matrix = block_table[:, :36].reshape(frame_count, 6, 6).transpose(1, 2, 0)
    right_side = block_table[:, 36:].T
    factor = {}
    for i in range(6):
        for j in range(i + 1):
            element = matrix[i, j]
            if i == j:
                element = element * (1.0 + LEVENBERG) + RIDGE
            for k in range(j):
                element = element - factor[i, k] * factor[j, k]
            factor[i, j] = jnp.sqrt(element) if i == j else element / factor[j, j]
    forward = []
    for i in range(6):
        element = right_side[i]
        for k in range(i):
            element = element - factor[i, k] * forward[k]
        forward.append(element / factor[i, i])
    result = [None] * 6
    for i in reversed(range(6)):
        element = forward[i]
        for k in range(i + 1, 6):
            element = element - factor[k, i] * result[k]
        result[i] = element / factor[i, i]
    return jnp.stack(result, 1)


def spread(values):
    nearby = with_halo(values[None], (("row", 0),), 1)
    return lax.all_gather(nearby, "col", axis=1, tiled=True)


def collect(buffer):
    col_part = lax.psum_scatter(buffer, "col", scatter_dimension=1, tiled=True)
    from_next = from_behind(col_part[0], "row", -1)
    from_prev = from_behind(col_part[2], "row", 1)
    return col_part[1] + from_next + from_prev


def shards(inv_depth, rotation, translation, edge_target, flow_obs, weight):
    frames_dev, pixels = inv_depth.shape
    per_frame = edge_target.shape[1]
    edges = frames_dev * per_frame
    columns = lax.axis_size("col")
    loop_size = lax.axis_size("row")
    group_size = frames_dev * columns
    total_frames = group_size * loop_size
    my_row = lax.axis_index("row")
    first_frame = (my_row * columns + lax.axis_index("col")) * frames_dev
    targets = edge_target.reshape(edges)
    sources = first_frame + jnp.arange(edges, dtype=jnp.int32) // per_frame
    offsets = (targets // group_size - my_row + 1 + loop_size) % loop_size
    slot_index = offsets * group_size + targets % group_size
    across, downward = pixel_grid(pixels)
    pose_parts = (
        lax.all_gather(rotation, ("row", "col"), axis=1, tiled=True),
        lax.all_gather(translation, ("row", "col"), axis=1, tiled=True),
    )
    pose_all = jnp.concatenate(pose_parts, 0)
    frame_ids = jnp.arange(total_frames, dtype=jnp.int32)
    src_hot = (sources[:, None] == frame_ids[None, :]).astype(jnp.float32)
    tgt_hot = (targets[:, None] == frame_ids[None, :]).astype(jnp.float32)
    pair_hot = src_hot - tgt_hot
    relative = jnp.dot(pair_hot, pose_all.T, precision=PRECISE).T
    nearby_depth = spread(inv_depth).reshape(3 * group_size, pixels)
    target_depth = jnp.take(nearby_depth, slot_index, axis=0)
    depth_grad, depth_curv, coupling, block, pose_grad = edge_terms(
        relative,
        target_depth,
        flow_obs.reshape(2, edges, pixels),
        weight.reshape(2, edges, pixels),
        across,
        downward,
    )
    slot_hot = (jnp.arange(3 * group_size, dtype=jnp.int32)[:, None] == slot_index[None, :]).astype(
        jnp.float32
    )

    def coalesce(values):
        flat_rows = values.reshape(edges, -1)
        summed = jnp.dot(slot_hot, flat_rows, precision=PRECISE)
        return summed.reshape((3, group_size) + values.shape[1:])

    depth_sums = collect(coalesce(jnp.stack([depth_grad, depth_curv], 1)))
    grad_sum = depth_sums[:, 0]
    inverse = 1.0 / (DAMP_DEPTH + depth_sums[:, 1])
    scaled = grad_sum * inverse
    returned = spread(jnp.stack([inverse, scaled], 1)).reshape(3 * group_size, 2, pixels)
    at_edges = jnp.take(returned, slot_index, axis=0)
    reduced = block - jnp.einsum(
        "aep,bep->eab", coupling * at_edges[:, 0][None], coupling, precision=PRECISE
    )
    reduced_grad = pose_grad - jnp.einsum("aep,ep->ea", coupling, at_edges[:, 1], precision=PRECISE)
    flat_block = reduced.reshape(edges, 36)
    out_rows = jnp.concatenate([flat_block, reduced_grad], 1)
    in_rows = jnp.concatenate([flat_block, -reduced_grad], 1)
    block_table = jnp.dot(src_hot.T, out_rows, precision=PRECISE) + jnp.dot(
        tgt_hot.T, in_rows, precision=PRECISE
    )
    block_table = lax.psum(block_table, ("row", "col"))
    frame_steps = solve_frames(block_table)
    own_step = lax.dynamic_slice_in_dim(frame_steps, first_frame, frames_dev, 0)
    motion = jnp.dot(pair_hot, frame_steps, precision=PRECISE)
    correction = jnp.einsum("aep,ea->ep", coupling, motion, precision=PRECISE)
    fix_sum = collect(coalesce(correction))
    depth_next = inv_depth + (grad_sum - fix_sum) * inverse
    return (depth_next, own_step.T)


def solution(mesh):
    return jax.shard_map(
        shards,
        mesh=mesh,
        in_specs=(
            P(("row", "col"), None),
            P(None, ("row", "col")),
            P(None, ("row", "col")),
            P(("row", "col"), None),
            P(None, ("row", "col"), None, None),
            P(None, ("row", "col"), None, None),
        ),
        out_specs=(P(("row", "col"), None), P(None, ("row", "col"))),
        check_vma=False,
    )
```

profile of v0, /device:TPU:0, one launch (start us, length us, event | category | flops | bytes accessed | tf_op | source)
XLA Modules:
  0.0 454.3 jit_solution(9152022826286836492)
XLA Ops:
  8.0 5.1 %collective-permute-start.1 = (f32[1,2,3072]{2,0,1:T(1,128)S(1)}, f32[1,2,3072]{2,0,1:T(1,128)S(1)}, u32[]{:S(2)}, u32[]{:S(2)}) collective-permute-start(f32[1,2,3072]{2,0,1:T(1,128)S(1)} %broadcast_in_dim.30), channel_id=1, source_target_pairs={{8,0},{16,8},{24,16},{0,24},{9,1},{17,9},{25,17},{1,25},{10,2},{18... | collective-permute-start | bytes 73736 | tf_op jit(solution)/shard_map/ppermute | solution.py:25
  17.0 42.3 %all-gather = f32[32,2,3]{2,1,0:T(2,128)S(1)} all-gather(f32[1,2,3]{2,1,0:T(2,128)} %bitcast.512), channel_id=1, replica_groups=mesh['row'=4,'col'=8] {'row','col'}, dimensions={0}, use_global_device_ids=true | all-gather | bytes 792 | tf_op jit(solution)/shard_map/all_gather | solution.py:150
  59.4 37.0 %all-gather.1 = f32[32,2,3]{2,1,0:T(2,128)S(1)} all-gather(f32[1,2,3]{2,1,0:T(2,128)} %bitcast.513), channel_id=1, replica_groups=mesh['row'=4,'col'=8] {'row','col'}, dimensions={0}, use_global_device_ids=true | all-gather | bytes 792 | tf_op jit(solution)/shard_map/all_gather | solution.py:151
  101.0 10.5 %all_gather.14 = f32[3,16,3072]{2,0,1:T(4,128)S(1)} all-gather(f32[3,2,3072]{2,0,1:T(4,128)S(1)} %pad_maximum_fusion.1), channel_id=1, replica_groups=mesh['row'=4,'col'=8] {'col'}, dimensions={1}, use_global_device_ids=true | all-gather | bytes 663552 | tf_op jit(solution)/shard_map/all_gather | solution.py:124
  112.8 2.0 multiply_dynamic-update-slice_fusion.3
  124.2 48.8 %all-reduce.5.cloned.1.call-done = f32[3,16,2,3072]{3,1,2,0:T(8,128)} async-done(((f32[3,16,2,3072]{3,1,2,0:T(8,128)}), f32[3,16,2,3072]{3,1,2,0:T(8,128)}) %all-reduce.5.cloned.1.call-update) | async-done | bytes 1179664
  174.0 3.3 collective-permute-start.2
  179.1 4.3 collective-permute-done.3
  184.6 2.0 collective-permute-start.4
  194.7 1.9 bitcast_subtract_fusion.1
  196.7 15.4 %all-gather.4.cloned.1.call-done = f32[3,16,2,3072]{3,2,0,1:T(2,128)} async-done(((f32[3,2,2,3072]{3,2,0,1:T(2,128)}), f32[3,16,2,3072]{3,2,0,1:T(2,128)}) %all-gather.4.cloned.1.call-update) | async-done | bytes 1179664 | tf_op jit(solution)/shard_map/all_gather | solution.py:124
  214.6 1.9 gather_fusion.1
  218.5 9.1 %broadcast_multiply_fusion = (f32[6,48,3072]{2,1,0:T(8,128)}, f32[6,48,3072]{2,1,0:T(8,128)S(1)}, f32[6,48,3072]{2,1,0:T(8,128)}, f32[6,48,3072]{2,1,0:T(8,128)}) fusion(f32[48,3072]{1,0:T(8,128)} %bitcast.500, f32[48,3072]{1,0:T(8,128)} %get-tuple-element.58, f32[48,3072]{1,0:T(8,128)} %get-tuple-element.55, ...), kind=kLoop, calls=%fused_computation.20 | loop fusion | flops 5308416 | bytes 24182784 | tf_op jit(solution)/shard_map/mul | solution.py:185
  227.6 12.9 %fusion.2 = f32[48,1,6]{2,1,0:T(1,128)} fusion(f32[6,48,3072]{2,1,0:T(8,128)S(1)} %get-tuple-element.39, f32[48,2,3072]{2,1,0:T(2,128)S(1)} %broadcast_select_fusion), kind=kOutput, calls=%fused_computation.4 | convolution fusion | flops 10616832 | bytes 4129920 | tf_op jit(solution)/shard_map/aep,ep->ea/dot_general | solution.py:187
  241.4 18.3 %fusion.8 = f32[48,6,6]{2,1,0:T(8,128)} fusion(f32[6,48,3072]{2,1,0:T(8,128)} %get-tuple-element.41, f32[6,48,3072]{2,1,0:T(8,128)} %get-tuple-element.60), kind=kOutput, calls=%fused_computation.10 | convolution fusion | flops 63700992 | bytes 7084800 | tf_op jit(solution)/shard_map/aep,bep->eab/dot_general | solution.py:85
  259.6 12.8 %fusion.6 = f32[48,1,6]{2,1,0:T(1,128)} fusion(f32[6,48,3072]{2,1,0:T(8,128)S(1)} %copy-done.1, f32[48,3072,1]{1,0,2:T(8,128)S(1)} %bitcast.502), kind=kOutput, calls=%fused_computation.8 | convolution fusion | flops 10616832 | bytes 4129920 | tf_op jit(solution)/shard_map/aep,ep->ea/dot_general | solution.py:88
  273.2 16.4 %fusion.19 = f32[48,6,6]{2,1,0:T(8,128)S(1)} fusion(f32[48,6,6]{2,1,0:T(8,128)} %fusion.8, f32[6,48,3072]{2,1,0:T(8,128)} %multiply_dynamic-update-slice_fusion.4, f32[6,48,3072]{2,1,0:T(8,128)} %get-tuple-element.40), kind=kOutput, calls=%fused_computation.28 | convolution fusion | flops 63702720 | bytes 7091712 | tf_op jit(solution)/shard_map/aep,bep->eab/dot_general | solution.py:85
  289.7 13.0 %fusion.10 = f32[48,1,6]{2,1,0:T(1,128)} fusion(f32[6,48,3072]{2,1,0:T(8,128)S(1)} %copy-done, f32[48,3072,1]{1,0,2:T(8,128)S(1)} %bitcast.501), kind=kOutput, calls=%fused_computation.12 | convolution fusion | flops 10616832 | bytes 4129920 | tf_op jit(solution)/shard_map/aep,ep->ea/dot_general | solution.py:88
  302.7 14.9 %fusion.24 = f32[48,6,6]{2,1,0:T(8,128)} fusion(f32[48,6,6]{2,1,0:T(8,128)S(1)} %fusion.19, f32[6,48,3072]{2,1,0:T(8,128)S(1)} %get-tuple-element.39, f32[6,48,3072]{2,1,0:T(8,128)S(1)} %copy-done.2), kind=kOutput, calls=%fused_computation.29 | convolution fusion | flops 63702720 | bytes 7091712 | tf_op jit(solution)/shard_map/aep,bep->eab/dot_general | solution.py:184
  324.0 39.9 %psum.7 = f32[64,42]{0,1:T(8,128)} all-reduce(f32[64,42]{0,1:T(8,128)} %convolution_add_fusion), channel_id=1, replica_groups=mesh['row'=4,'col'=8] {'row','col'}, use_global_device_ids=true, to_apply=%region_1.2 | all-reduce | flops 2688 | bytes 21504 | tf_op jit(solution)/shard_map/psum | solution.py:194
  372.2 6.0 %fusion = f32[48,1,3072]{2,1,0:T(1,128)S(1)} fusion(f32[48,6,1]{1,2,0:T(1,128)S(1)} %bitcast.509, f32[6,48,3072]{2,1,0:T(8,128)S(1)} %get-tuple-element.39), kind=kOutput, calls=%fused_computation.2 | convolution fusion | flops 10616832 | bytes 4129920 | tf_op jit(solution)/shard_map/aep,ea->ep/dot_general | solution.py:198
  379.6 56.4 %all-reduce.7.cloned.1.call-done = f32[3,16,3072]{2,1,0:T(8,128)} async-done(((f32[3,16,3072]{2,1,0:T(8,128)}), f32[3,16,3072]{2,1,0:T(8,128)}) %all-reduce.7.cloned.1.call-update) | async-done | bytes 589840
  436.9 3.3 collective-permute-start.6
  441.7 4.1 collective-permute-done.7
  (125 shorter events, 57.4 us)
Async XLA Ops:
  7.2 92.5 %copy-start.21 = (u32[32]{0:T(128)S(1)}, u32[32]{0:T(128)}, u32[]{:S(2)}) copy-start(u32[32]{0:T(128)} %constant.161) | copy-start | bytes 388
  7.2 165.8 %all-reduce.5.cloned.1.call-start = ((), (), s32[]{:S(2)}) async-start(), calls=%async_computation.1 | async-start | bytes 2359296
  8.0 93.0 %collective-permute-start.1 = (f32[1,2,3072]{2,0,1:T(1,128)S(1)}, f32[1,2,3072]{2,0,1:T(1,128)S(1)}, u32[]{:S(2)}, u32[]{:S(2)}) collective-permute-start(f32[1,2,3072]{2,0,1:T(1,128)S(1)} %broadcast_in_dim.30), channel_id=1, source_target_pairs={{8,0},{16,8},{24,16},{0,24},{9,1},{17,9},{25,17},{1,25},{10,2},{18... | collective-permute-start | bytes 73736 | tf_op jit(solution)/shard_map/ppermute | solution.py:25
  13.1 87.8 %collective-permute-start = (f32[1,2,3072]{2,0,1:T(1,128)S(1)}, f32[1,2,3072]{2,0,1:T(1,128)S(1)}, u32[]{:S(2)}, u32[]{:S(2)}) collective-permute-start(f32[1,2,3072]{2,0,1:T(1,128)S(1)} %broadcast_in_dim.30), channel_id=1, source_target_pairs={{0,8},{8,16},{16,24},{24,0},{1,9},{9,17},{17,25},{25,1},{2,10},{10... | collective-permute-start | bytes 73736 | tf_op jit(solution)/shard_map/ppermute | solution.py:23
  13.9 98.0 %copy-start.20 = (s32[48]{0:T(128)}, s32[48]{0:T(128)S(1)}, u32[]{:S(2)}) copy-start(s32[48]{0:T(128)S(1)} %reshape.5243) | copy-start | bytes 580
  15.9 96.1 %copy-start.22 = (s32[48]{0:T(128)}, s32[48]{0:T(128)S(1)}, u32[]{:S(2)}) copy-start(s32[48]{0:T(128)S(1)} %fusion.82) | copy-start | bytes 580
  99.0 15.8 %copy-start.3 = (f32[1,2,24,3072]{3,2,1,0:T(8,128)}, f32[1,2,24,3072]{3,2,1,0:T(8,128)S(1)}, u32[]{:S(2)}) copy-start(f32[1,2,24,3072]{3,2,1,0:T(8,128)S(1)} %get-tuple-element.72) | copy-start | bytes 1769476
  99.0 15.8 %copy-start.4 = (f32[1,2,24,3072]{3,2,1,0:T(8,128)}, f32[1,2,24,3072]{3,2,1,0:T(8,128)S(1)}, u32[]{:S(2)}) copy-start(f32[1,2,24,3072]{3,2,1,0:T(8,128)S(1)} %get-tuple-element.73) | copy-start | bytes 1769476
  116.5 6.3 %copy-start.16 = (f32[48]{0:T(128)S(1)}, f32[48]{0:T(128)}, u32[]{:S(2)}) copy-start(f32[48]{0:T(128)} %get-tuple-element.67) | copy-start | bytes 580
  118.3 93.7 %all-gather.4.cloned.1.call-start = ((), (), s32[]{:S(2)}) async-start(), calls=%async_computation | async-start | bytes 1327104 | tf_op jit(solution)/shard_map/all_gather | solution.py:124
  119.7 66.9 %copy-start.13 = (f32[3072]{0:T(1024)S(1)}, f32[3072]{0:T(1024)}, u32[]{:S(2)}) copy-start(f32[3072]{0:T(1024)} %fusion.76) | copy-start | bytes 36868
  174.0 5.1 %collective-permute-start.2 = (f32[2,2,3072]{2,0,1:T(2,128)S(1)}, f32[2,2,3072]{2,0,1:T(2,128)S(1)}, u32[]{:S(2)}, u32[]{:S(2)}) collective-permute-start(f32[2,2,3072]{2,0,1:T(2,128)S(1)} %get-tuple-element.48), channel_id=1, source_target_pairs={{0,24},{8,0},{16,8},{24,16},{1,25},{9,1},{17,9},{25,17},{2,26},{10... | collective-permute-start | bytes 147464 | tf_op jit(solution)/shard_map/ppermute | solution.py:34
  177.3 6.1 %collective-permute-start.3 = (f32[2,2,3072]{2,0,1:T(2,128)S(1)}, f32[2,2,3072]{2,0,1:T(2,128)S(1)}, u32[]{:S(2)}, u32[]{:S(2)}) collective-permute-start(f32[2,2,3072]{2,0,1:T(2,128)S(1)} %get-tuple-element.49), channel_id=1, source_target_pairs={{0,8},{8,16},{16,24},{24,0},{1,9},{9,17},{17,25},{25,1},{2,10},{10... | collective-permute-start | bytes 147464 | tf_op jit(solution)/shard_map/ppermute | solution.py:34
  184.5 4.1 collective-permute-start.5
  184.6 5.9 %collective-permute-start.4 = (f32[1,2,2,3072]{3,1,2,0:T(2,128)S(1)}, f32[1,2,2,3072]{3,1,2,0:T(2,128)S(1)}, u32[]{:S(2)}, u32[]{:S(2)}) collective-permute-start(f32[1,2,2,3072]{3,1,2,0:T(2,128)S(1)} %maximum_bitcast_fusion.1), channel_id=1, source_target_pairs={{0,8},{8,16},{16,24},{24,0},{1,9},{9,17},{17,25},{25,1},{2,10},{10... | collective-permute-start | bytes 147464 | tf_op jit(solution)/shard_map/ppermute | solution.py:23
  191.3 244.6 %all-reduce.7.cloned.1.call-start = ((), (), s32[]{:S(2)}) async-start(), calls=%async_computation.2 | async-start | bytes 1179648
  241.4 18.3 %copy-start.1 = (f32[6,48,3072]{2,1,0:T(8,128)S(1)}, f32[6,48,3072]{2,1,0:T(8,128)}, u32[]{:S(2)}) copy-start(f32[6,48,3072]{2,1,0:T(8,128)} %get-tuple-element.41) | copy-start | bytes 10616836
  241.4 18.3 %copy-start.6 = (f32[48,3072]{1,0:T(8,128)S(1)}, f32[48,3072]{1,0:T(8,128)}, u32[]{:S(2)}) copy-start(f32[48,3072]{1,0:T(8,128)} %get-tuple-element.59) | copy-start | bytes 1769476
  273.2 16.5 %copy-start = (f32[6,48,3072]{2,1,0:T(8,128)S(1)}, f32[6,48,3072]{2,1,0:T(8,128)}, u32[]{:S(2)}) copy-start(f32[6,48,3072]{2,1,0:T(8,128)} %get-tuple-element.40) | copy-start | bytes 10616836
  273.2 16.5 %copy-start.5 = (f32[48,3072]{1,0:T(8,128)S(1)}, f32[48,3072]{1,0:T(8,128)}, u32[]{:S(2)}) copy-start(f32[48,3072]{1,0:T(8,128)} %get-tuple-element.54) | copy-start | bytes 1769476
  289.7 13.0 %copy-start.2 = (f32[6,48,3072]{2,1,0:T(8,128)S(1)}, f32[6,48,3072]{2,1,0:T(8,128)}, u32[]{:S(2)}) copy-start(f32[6,48,3072]{2,1,0:T(8,128)} %get-tuple-element.38) | copy-start | bytes 10616836
  317.6 60.6 %copy-start.19 = (s32[48]{0:T(128)S(1)}, s32[48]{0:T(128)}, u32[]{:S(2)}) copy-start(s32[48]{0:T(128)} %get-tuple-element.45) | copy-start | bytes 580
  436.9 4.8 %collective-permute-start.6 = (f32[2,3072]{1,0:T(2,128)S(1)}, f32[2,3072]{1,0:T(2,128)S(1)}, u32[]{:S(2)}, u32[]{:S(2)}) collective-permute-start(f32[2,3072]{1,0:T(2,128)S(1)} %get-tuple-element.62), channel_id=1, source_target_pairs={{0,24},{8,0},{16,8},{24,16},{1,25},{9,1},{17,9},{25,17},{2,26},{10... | collective-permute-start | bytes 73736 | tf_op jit(solution)/shard_map/ppermute | solution.py:34
  440.2 5.6 %collective-permute-start.7 = (f32[2,3072]{1,0:T(2,128)S(1)}, f32[2,3072]{1,0:T(2,128)S(1)}, u32[]{:S(2)}, u32[]{:S(2)}) collective-permute-start(f32[2,3072]{1,0:T(2,128)S(1)} %get-tuple-element.63), channel_id=1, source_target_pairs={{0,8},{8,16},{16,24},{24,0},{1,9},{9,17},{17,25},{25,1},{2,10},{10... | collective-permute-start | bytes 73736 | tf_op jit(solution)/shard_map/ppermute | solution.py:34
  (10 other events, 27.4 us)
Sparse Core Ops, SparseCore 0:
  118.4 54.4 all-reduce.4
  191.5 20.5 all-gather.3
  379.7 56.1 all-reduce.6
where the time goes:
time: 461 us; the launch traced here: 454 us
  waiting for transfers between devices  133 us (29%)
  blocking collectives  130 us (28%)
  matrix products  101 us (22%)
  other arithmetic  33.8 us (7%)
  local copies, waits for them, and re-layouts  27.4 us (6%)
  between operations  15.2 us (3%)
  starting transfers between devices  14.1 us (3%)
    unnamed x5, waiting for transfers between devices  105 us
    all_gather x1, blocking collectives, shards(): lax.all_gather(rotation, ('row', 'col'), axis=1, tiled=True)  42.3 us
    psum x1, blocking collectives, shards(): block_table = lax.psum(block_table, ('row', 'col'))  39.9 us
    all_gather x1, blocking collectives, shards(): lax.all_gather(translation, ('row', 'col'), axis=1, tiled=True)  37 us
    dot_general x1, matrix products, edge_terms(): jnp.einsum('aep,bep->eab', scaled_v, jac_v, precision=PRECISE)  18.3 us
    dot_general x1, matrix products, edge_terms(): jnp.einsum('aep,bep->eab', scaled_u, jac_u, precision=PRECISE)  16.4 us
    all_gather x1, waiting for transfers between devices, spread(): return lax.all_gather(nearby, 'col', axis=1, tiled=True)  15.4 us
    dot_general x1, matrix products, shards(): jnp.einsum('aep,bep->eab', coupling * at_edges[:, 0][None], coupling, pre...  14.9 us
  transfers between devices with their start and end apart: 11, of which 9 were waited for; matrix products, arithmetic and copies ran while one was open for 5% of the time, Pallas kernels for 0%

commit v1 on v0

v1 whole, which is shorter than its diff:
```python
import functools

import jax
import jax.numpy as jnp
from jax import lax
from jax.experimental import pallas as pl
from jax.experimental.pallas import tpu as pltpu
from jax.sharding import PartitionSpec as P

IMG_H = 48
IMG_W = 64
DAMP_DEPTH = 0.1
LEVENBERG = 0.1
RIDGE = 0.001
TAIL = 8
LANES = 128
PAIRS = [(i, j) for i in range(6) for j in range(i + 1)]
U_AXES = (0, 1, 2, 3, 5)
V_AXES = (0, 1, 2, 4, 5)
F32 = jnp.float32
BF16 = jnp.bfloat16


def split3(x):
    high = x.astype(BF16)
    rest = x - high.astype(F32)
    mid = rest.astype(BF16)
    low = (rest - mid.astype(F32)).astype(BF16)
    return high, mid, low


def pick(hot, parts, dims=((1,), (0,))):
    hot = hot.astype(BF16)
    total = None
    for part in reversed(parts):
        term = lax.dot_general(hot, part, (dims, ((), ())), preferred_element_type=F32)
        total = term if total is None else total + term
    return total


def lane_tiles(width):
    step = LANES if width % LANES == 0 else width
    return [(start, step) for start in range(0, width, step)]


def as_column(row, count):
    across = lax.broadcasted_iota(jnp.int32, (count, count), 1)
    down = lax.broadcasted_iota(jnp.int32, (count, count), 0)
    return jnp.sum(jnp.where(across == down, row, 0.0), axis=1, keepdims=True)


def source_local(device, count, per_frame, frames_dev, shape, axis):
    edge = lax.broadcasted_iota(jnp.int32, shape, axis)
    frame = jnp.zeros(shape, jnp.int32)
    for k in range(1, frames_dev):
        frame = frame + (edge >= k * per_frame).astype(jnp.int32)
    return frame + device * frames_dev


def as_hot(test):
    return jnp.where(test, 1.0, 0.0).astype(F32)


def pack_kernel(dims, flow, weight, depth, aux, out):
    frames_dev, per_frame, width = dims
    edges = frames_dev * per_frame
    for part, ref in enumerate((flow, weight)):
        for comp in range(2):
            for f in range(frames_dev):
                row = (part * 2 + comp) * edges + f * per_frame
                out[0, row : row + per_frame, :] = ref[comp, f, :, :]
    base = 4 * edges
    out[0, base : base + TAIL, :] = aux[...]
    out[0, base : base + frames_dev, :] = depth[...]


def table_kernel(dims, tails, out):
    frames_dev, per_frame, width = dims
    devices = tails.shape[0]
    for d in range(devices):
        for f in range(frames_dev):
            row = d * frames_dev + f
            out[0, row : row + 1, :] = tails[d, f : f + 1, :]
            out[1, row : row + 1, :] = tails[d, frames_dev + f : frames_dev + f + 1, :]


def first_kernel(dims, slot_row, slot_col, rays, block, own, prev, following, gc_prev, gc_own, gc_next, maps, sums, depth3, pose3, acc):
    frames_dev, per_frame, width, group = dims
    edges = frames_dev * per_frame
    d = pl.program_id(0)

    @pl.when(d == 0)
    def _():
        for b, ref in enumerate((prev, own, following)):
            for k, part in enumerate(split3(ref[0])):
                depth3[k, b * group : (b + 1) * group, :] = part
            for k, part in enumerate(split3(ref[1])):
                pose3[k, b * group : (b + 1) * group, :] = part
        acc[...] = jnp.zeros_like(acc)

    base = 4 * edges
    target_row = block[0, base + 2 * frames_dev : base + 2 * frames_dev + 1, 0:edges]
    target_col = as_column(target_row, edges)
    slots = 3 * group
    hot = as_hot(target_col == slot_row[...])
    hot_t = as_hot(slot_col[...] == target_row)
    local = source_local(d, edges, per_frame, frames_dev, (edges, slots), 0)
    src = as_hot(lax.broadcasted_iota(jnp.int32, (edges, slots), 1) == local + group)
    target_depth = pick(hot, [depth3[k] for k in range(3)])
    relative = pick(src - hot, [pose3[k] for k in range(3)])
    grads, curvs = [], []
    for g in range(0, edges, 8):
        rel = relative[g : g + 8, :]
        w0, w1, w2, m0, m1, m2 = [rel[:, i : i + 1] for i in range(6)]
        partial = {}
        grad_row, curv_row = [], []
        for start, step in lane_tiles(width):
            lanes = slice(start, start + step)
            x = rays[0:1, lanes]
            y = rays[1:2, lanes]
            dep = target_depth[g : g + 8, lanes]
            f0 = block[0, g : g + 8, lanes]
            f1 = block[0, edges + g : edges + g + 8, lanes]
            cu = block[0, 2 * edges + g : 2 * edges + g + 8, lanes]
            cv = block[0, 3 * edges + g : 3 * edges + g + 8, lanes]
            x0 = x + w1 - w2 * y + m0 * dep
            x1 = y + w2 * x - w0 + m1 * dep
            x2 = 1.0 + w0 * y - w1 * x + m2 * dep
            q = 1.0 / x2
            u = x0 * q
            v = x1 * q
            ru = f0 - (u - x)
            rv = f1 - (v - y)
            du = q * (m0 - u * m2)
            dv = q * (m1 - v * m2)
            dq = dep * q
            uq = u * q
            vq = v * q
            ju = {0: -y * uq, 1: q + x * uq, 2: -y * q, 3: dq, 5: -u * dq}
            jv = {0: -q - y * vq, 1: x * vq, 2: x * q, 4: dq, 5: -v * dq}
            cud = cu * du
            cvd = cv * dv
            grad_row.append(cud * ru + cvd * rv)
            curv_row.append(cud * du + cvd * dv)
            for a in range(6):
                term = None
                if a in ju:
                    term = cud * ju[a]
                if a in jv:
                    term = cvd * jv[a] if term is None else term + cvd * jv[a]
                maps[0, a, g : g + 8, lanes] = term
            su = {a: cu * ju[a] for a in ju}
            sv = {a: cv * jv[a] for a in jv}

            def add(key, value):
                partial[key] = value if key not in partial else partial[key] + value

            for k, (a, b) in enumerate(PAIRS):
                if a in ju and b in ju:
                    add(k, su[a] * ju[b])
                if a in jv and b in jv:
                    add(k, sv[a] * jv[b])
            for a in range(6):
                if a in ju:
                    add(21 + a, su[a] * ru)
                if a in jv:
                    add(21 + a, sv[a] * rv)
        grads.append(grad_row)
        curvs.append(curv_row)
        lane = lax.broadcasted_iota(jnp.int32, (8, LANES), 1)
        packed = jnp.zeros((8, LANES), F32)
        for k in sorted(partial):
            packed = jnp.where(lane == k, jnp.sum(partial[k], axis=1, keepdims=True), packed)
        sums[g : g + 8, :] = packed

    for index, rows in enumerate((grads, curvs)):
        for t, (start, step) in enumerate(lane_tiles(width)):
            value = jnp.concatenate([row[t] for row in rows], axis=0)
            acc[index, :, start : start + step] += pick(hot_t, split3(value))

    @pl.when(d == pl.num_programs(0) - 1)
    def _():
        gc_prev[...] = acc[:, 0:group, :]
        gc_own[...] = acc[:, group : 2 * group, :]
        gc_next[...] = acc[:, 2 * group : 3 * group, :]


def second_kernel(dims, slot_row, first, tails, maps, sums, prev, own, following, table, back3, acc):
    frames_dev, per_frame, width, group, frames = dims
    edges = frames_dev * per_frame
    d = pl.program_id(0)

    @pl.when(d == 0)
    def _():
        for b, ref in enumerate((prev, own, following)):
            for i in range(2):
                for k, part in enumerate(split3(ref[i])):
                    back3[i, k, b * group : (b + 1) * group, :] = part
        acc[...] = jnp.zeros_like(acc)

    target_row = tails[0, 2 * frames_dev : 2 * frames_dev + 1, 0:edges]
    target_col = as_column(target_row, edges)
    hot = as_hot(target_col == slot_row[...])
    inverse = pick(hot, [back3[0, k] for k in range(3)])
    scaled = pick(hot, [back3[1, k] for k in range(3)])
    rows = []
    for g in range(0, edges, 8):
        partial = {}
        for start, step in lane_tiles(width):
            lanes = slice(start, start + step)
            inv = inverse[g : g + 8, lanes]
            sca = scaled[g : g + 8, lanes]
            e = [maps[0, a, g : g + 8, lanes] for a in range(6)]
            ei = [value * inv for value in e]

            def add(key, value):
                partial[key] = value if key not in partial else partial[key] + value

            for k, (a, b) in enumerate(PAIRS):
                add(k, ei[a] * e[b])
            for a in range(6):
                add(21 + a, e[a] * sca)
        lane = lax.broadcasted_iota(jnp.int32, (8, LANES), 1)
        packed = jnp.zeros((8, LANES), F32)
        for k in sorted(partial):
            packed = jnp.where(lane == k, jnp.sum(partial[k], axis=1, keepdims=True), packed)
        rows.append(sums[g : g + 8, :] - packed)
    edge_rows = split3(jnp.concatenate(rows, axis=0))
    ids = lax.broadcasted_iota(jnp.int32, (frames, edges), 0)
    local = source_local(d, edges, per_frame, frames_dev, (frames, edges), 1)
    src_t = as_hot(ids == local + first[0])
    tgt_t = as_hot(ids.astype(F32) == target_row)
    plus = pick(src_t + tgt_t, edge_rows)
    minus = pick(src_t - tgt_t, edge_rows)
    lane = lax.broadcasted_iota(jnp.int32, (frames, LANES), 1)
    acc[...] += jnp.where(lane < 21, plus, minus)

    @pl.when(d == pl.num_programs(0) - 1)
    def _():
        table[...] = acc[...].T[0 : table.shape[0], :]


def solve_rows(entry):
    factor = {}
    scale = {}
    for i in range(6):
        for j in range(i + 1):
            element = entry(PAIRS.index((i, j)))
            if i == j:
                element = element * (1.0 + LEVENBERG) + RIDGE
            for k in range(j):
                element = element - factor[i, k] * factor[j, k]
            if i == j:
                factor[i, j] = jnp.sqrt(element)
                scale[i] = 1.0 / factor[i, j]
            else:
                factor[i, j] = element * scale[j]
    forward = []
    for i in range(6):
        element = entry(21 + i)
        for k in range(i):
            element = element - factor[i, k] * forward[k]
        forward.append(element * scale[i])
    result = [None] * 6
    for i in reversed(range(6)):
        element = forward[i]
        for k in range(i + 1, 6):
            element = element - factor[k, i] * result[k]
        result[i] = element * scale[i]
    return result


def third_kernel(dims, slot_col, first, tails, maps, *refs):
    frames_dev, per_frame, width, group, frames, count = dims
    tables = refs[:count]
    z_prev, z_own, z_next, step_out, step3, acc = refs[count:]
    edges = frames_dev * per_frame
    d = pl.program_id(0)

    @pl.when(d == 0)
    def _():
        total = tables[0][...]
        for ref in tables[1:]:
            total = total + ref[...]
        result = solve_rows(lambda k: total[k : k + 1, :])
        stacked = jnp.concatenate(result + [jnp.zeros((2, frames), F32)], axis=0)
        step_out[...] = stacked
        for k, part in enumerate(split3(stacked)):
            step3[k] = part
        acc[...] = jnp.zeros_like(acc)

    target_row = tails[0, 2 * frames_dev : 2 * frames_dev + 1, 0:edges]
    target_col = as_column(target_row, edges)
    hot_t = as_hot(slot_col[...] == target_row)
    ids = lax.broadcasted_iota(jnp.int32, (edges, frames), 1)
    local = source_local(d, edges, per_frame, frames_dev, (edges, frames), 0)
    pair = as_hot(ids == local + first[0]) - as_hot(ids.astype(F32) == target_col)
    motion = pick(pair, [step3[k] for k in range(3)], ((1,), (1,)))
    blocks = []
    for g in range(0, edges, 8):
        move = [motion[g : g + 8, a : a + 1] for a in range(6)]
        row = []
        for start, step in lane_tiles(width):
            lanes = slice(start, start + step)
            value = maps[0, 0, g : g + 8, lanes] * move[0]
            for a in range(1, 6):
                value = value + maps[0, a, g : g + 8, lanes] * move[a]
            row.append(value)
        blocks.append(row)
    for t, (start, step) in enumerate(lane_tiles(width)):
        value = jnp.concatenate([row[t] for row in blocks], axis=0)
        acc[:, start : start + step] += pick(hot_t, split3(value))

    @pl.when(d == pl.num_programs(0) - 1)
    def _():
        z_prev[...] = acc[0:group, :]
        z_own[...] = acc[group : 2 * group, :]
        z_next[...] = acc[2 * group : 3 * group, :]


def shift(values, axis, by):
    count = lax.axis_size(axis)
    return lax.ppermute(values, axis, [(i, (i + by) % count) for i in range(count)])


def chip_partner(values, step):
    count = lax.axis_size("col")
    chips = count // 2
    pairs = []
    for i in range(count):
        chip, core = i // 2, i % 2
        other = chip ^ step if chips & (chips - 1) == 0 else (chip + step) % chips
        pairs.append((i, other * 2 + core))
    return lax.ppermute(values, "col", pairs)


def core_partner(values):
    count = lax.axis_size("col")
    return lax.ppermute(values, "col", [(i, i ^ 1) for i in range(count)])


def whole(shape):
    return pl.BlockSpec(shape, lambda d: (0,) * len(shape))


def params():
    return pltpu.CompilerParams(dimension_semantics=("arbitrary",), vmem_limit_bytes=24 * 1024 * 1024)


def pack_blocks(flow_obs, weight, inv_depth, aux, columns):
    frames_dev, pixels = inv_depth.shape
    per_frame = flow_obs.shape[2]
    edges = frames_dev * per_frame
    width = pixels // columns
    rows = 4 * edges + TAIL
    if width % LANES:
        def cut(values):
            return values.reshape(-1, columns, width).transpose(1, 0, 2)

        tail = jnp.broadcast_to(aux[None, frames_dev:], (columns, TAIL - frames_dev, width))
        return jnp.concatenate([cut(flow_obs), cut(weight), cut(inv_depth), tail], axis=1)
    return pl.pallas_call(
        functools.partial(pack_kernel, (frames_dev, per_frame, width)),
        grid=(columns,),
        in_specs=[
            pl.BlockSpec((2, frames_dev, per_frame, width), lambda j: (0, 0, 0, j)),
            pl.BlockSpec((2, frames_dev, per_frame, width), lambda j: (0, 0, 0, j)),
            pl.BlockSpec((frames_dev, width), lambda j: (0, j)),
            whole((TAIL, width)),
        ],
        out_specs=pl.BlockSpec((1, rows, width), lambda j: (j, 0, 0)),
        out_shape=jax.ShapeDtypeStruct((columns, rows, width), F32),
        compiler_params=params(),
        name="pack",
    )(flow_obs, weight, inv_depth, aux)


def shards(inv_depth, rotation, translation, edge_target, flow_obs, weight):
    frames_dev, pixels = inv_depth.shape
    per_frame = edge_target.shape[1]
    edges = frames_dev * per_frame
    columns = lax.axis_size("col")
    loop_size = lax.axis_size("row")
    group = frames_dev * columns
    frames = group * loop_size
    slots = 3 * group
    width = pixels // columns
    rows = 4 * edges + TAIL
    my_row = lax.axis_index("row")
    my_col = lax.axis_index("col")
    first = (my_row * group).astype(jnp.int32).reshape(1)

    pose = jnp.concatenate([rotation, translation], 0).T
    aux = jnp.concatenate(
        [
            jnp.zeros((frames_dev, width), F32),
            jnp.pad(pose, ((0, 0), (0, width - 6))),
            jnp.pad(edge_target.astype(F32).reshape(1, edges), ((0, 0), (0, width - edges))),
            jnp.zeros((TAIL - 2 * frames_dev - 1, width), F32),
        ],
        0,
    )
    packed = pack_blocks(flow_obs, weight, inv_depth, aux, columns)
    blocks = lax.all_to_all(packed, "col", 0, 0, tiled=True)

    tails_spec = pl.BlockSpec((columns, TAIL, width), lambda d: (0, 4 * edges // TAIL, 0))
    own_table = pl.pallas_call(
        functools.partial(table_kernel, (frames_dev, per_frame, width)),
        grid=(1,),
        in_specs=[tails_spec],
        out_specs=whole((2, group, width)),
        out_shape=jax.ShapeDtypeStruct((2, group, width), F32),
        compiler_params=params(),
        name="gather_table",
    )(blocks)
    prev_table = shift(own_table, "row", 1)
    next_table = shift(own_table, "row", -1)

    slot = jnp.arange(slots, dtype=jnp.int32)
    slot_id = ((my_row - 1 + slot // group + loop_size) % loop_size) * group + slot % group
    slot_row = slot_id.astype(F32).reshape(1, slots)
    slot_col = slot_id.astype(F32).reshape(slots, 1)
    index = my_col * width + jnp.arange(width, dtype=jnp.int32)
    across = (index % IMG_W).astype(F32)
    downward = (index // IMG_W).astype(F32)
    rays = jnp.stack([(across + 0.5) / IMG_W - 0.5, (downward + 0.5 - 0.5 * IMG_H) / IMG_W])

    smem = pl.BlockSpec(memory_space=pltpu.SMEM)
    one_tail = pl.BlockSpec((1, TAIL, width), lambda d: (d, 4 * edges // TAIL, 0))
    maps_spec = pl.BlockSpec((1, 6, edges, width), lambda d: (d, 0, 0, 0))
    sums_spec = pl.BlockSpec((edges, LANES), lambda d: (d, 0))
    pair_shape = jax.ShapeDtypeStruct((2, group, width), F32)
    gc_prev, gc_own, gc_next, maps, sums = pl.pallas_call(
        functools.partial(first_kernel, (frames_dev, per_frame, width, group)),
        grid=(columns,),
        in_specs=[
            whole((1, slots)),
            whole((slots, 1)),
            whole((2, width)),
            pl.BlockSpec((1, rows, width), lambda d: (d, 0, 0)),
        ]
        + [whole((2, group, width))] * 3,
        out_specs=[whole((2, group, width))] * 3 + [maps_spec, sums_spec],
        out_shape=[pair_shape] * 3
        + [
            jax.ShapeDtypeStruct((columns, 6, edges, width), F32),
            jax.ShapeDtypeStruct((columns * edges, LANES), F32),
        ],
        scratch_shapes=[
            pltpu.VMEM((3, slots, width), BF16),
            pltpu.VMEM((3, slots, width), BF16),
            pltpu.VMEM((2, slots, width), F32),
        ],
        compiler_params=params(),
        name="first_pass",
    )(slot_row, slot_col, rays, blocks, own_table, prev_table, next_table)

    sums_gc = gc_own + shift(gc_next, "row", 1) + shift(gc_prev, "row", -1)
    grad_sum = sums_gc[0]
    inverse = 1.0 / (DAMP_DEPTH + sums_gc[1])
    back_own = jnp.stack([inverse, grad_sum * inverse])
    back_prev = shift(back_own, "row", 1)
    back_next = shift(back_own, "row", -1)

    table = pl.pallas_call(
        functools.partial(second_kernel, (frames_dev, per_frame, width, group, frames)),
        grid=(columns,),
        in_specs=[whole((1, slots)), smem, one_tail, maps_spec, sums_spec] + [whole((2, group, width))] * 3,
        out_specs=whole((32, frames)),
        out_shape=jax.ShapeDtypeStruct((32, frames), F32),
        scratch_shapes=[pltpu.VMEM((2, 3, slots, width), BF16), pltpu.VMEM((frames, LANES), F32)],
        compiler_params=params(),
        name="second_pass",
    )(slot_row, first, blocks, maps, sums, back_prev, back_own, back_next)

    arrived = [chip_partner(table, step) for step in range(1, columns // 2)]
    for value in arrived:
        table = table + value
    table = table + core_partner(table)
    tables = [table] + [shift(table, "row", by) for by in range(1, loop_size)]

    z_shape = jax.ShapeDtypeStruct((group, width), F32)
    z_prev, z_own, z_next, step = pl.pallas_call(
        functools.partial(third_kernel, (frames_dev, per_frame, width, group, frames, loop_size)),
        grid=(columns,),
        in_specs=[whole((slots, 1)), smem, one_tail, maps_spec] + [whole((32, frames))] * loop_size,
        out_specs=[whole((group, width))] * 3 + [whole((8, frames))],
        out_shape=[z_shape] * 3 + [jax.ShapeDtypeStruct((8, frames), F32)],
        scratch_shapes=[pltpu.VMEM((3, 8, frames), BF16), pltpu.VMEM((slots, width), F32)],
        compiler_params=params(),
        name="third_pass",
    )(slot_col, first, blocks, maps, *tables)

    fix = z_own + shift(z_next, "row", 1) + shift(z_prev, "row", -1)
    depth_chunk = own_table[0] + (grad_sum - fix) * inverse
    gathered = lax.all_to_all(depth_chunk.reshape(columns, frames_dev, width), "col", 0, 0, tiled=True)
    depth_next = gathered.transpose(1, 0, 2).reshape(frames_dev, pixels)
    first_own = (my_row * columns + my_col) * frames_dev
    pose_step = lax.dynamic_slice(step, (0, first_own), (6, frames_dev))
    return depth_next, pose_step


def solution(mesh):
    return jax.shard_map(
        shards,
        mesh=mesh,
        in_specs=(
            P(("row", "col"), None),
            P(None, ("row", "col")),
            P(None, ("row", "col")),
            P(("row", "col"), None),
            P(None, ("row", "col"), None, None),
            P(None, ("row", "col"), None, None),
        ),
        out_specs=(P(("row", "col"), None), P(None, ("row", "col"))),
        check_vma=False,
    )
```

time: 461 us -> 119 us (0.26); the launches traced: 454 us -> 119 us
  blocking collectives: 130 us -> 0 us
  matrix products: 101 us -> 0 us
  waiting for transfers between devices: 133 us -> 57.4 us
  other arithmetic: 33.8 us -> 1.66 us
  Pallas kernels: 0 us -> 18.6 us
  local copies, waits for them, and re-layouts: 27.4 us -> 10.6 us
  starting transfers between devices: 14.1 us -> 29.6 us
  between operations: 15.2 us -> 0.77 us
    unnamed x5 -> x0, waiting for transfers between devices: 105 us -> none
    dot_general x13 -> x0, matrix products: 101 us -> none  [the longest x1 18.3 us: edge_terms(): jnp.einsum('aep,bep->eab', scaled_v, jac_v, precision=PRECISE)]
    all_gather x3 -> x0, blocking collectives: 89.8 us -> none  [the longest x1 42.3 us: shards(): lax.all_gather(rotation, ('row', 'col'), axis=1, tiled=True)]
    psum x1 -> x0, blocking collectives: 39.9 us -> none  [shards(): block_table = lax.psum(block_table, ('row', 'col'))]
    all_to_all x0 -> x2, waiting for transfers between devices: none -> 34.4 us  [the longest x1 30.4 us: shards(): blocks = lax.all_to_all(packed, 'col', 0, 0, tiled=True)]
    pallas_call x0 -> x5, Pallas kernels: none -> 18.6 us  [the longest x1 7.74 us: shards(): pl.pallas_call(functools.partial(first_kernel, (frames_dev, per_frame, wi...]
    all_gather x1 -> x0, waiting for transfers between devices: 15.4 us -> none  [spread(): return lax.all_gather(nearby, 'col', axis=1, tiled=True)]
    ppermute x8 -> x15, waiting for transfers between devices: 12.6 us -> 23 us  [the longest x11 20.1 us: shift(): lax.ppermute(values, axis, [(i, (i + by) % count) for i in range(count)])]
  transfers between devices with their start and end apart: 11 -> 17, of which waited for: 9 -> 14; matrix products, arithmetic and copies ran while one was open for 5% -> 1% of each run, Pallas kernels for 0% -> 0%
where the time goes in v1:
time: 119 us
  waiting for transfers between devices  57.4 us (48%)
  starting transfers between devices  29.6 us (25%)
  Pallas kernels  18.6 us (16%)
  local copies, waits for them, and re-layouts  10.6 us (9%)
  other arithmetic  1.66 us (1%)
    all_to_all x1, waiting for transfers between devices, shards(): blocks = lax.all_to_all(packed, 'col', 0, 0, tiled=True)  30.4 us
    ppermute x11, waiting for transfers between devices, shift(): lax.ppermute(values, axis, [(i, (i + by) % count) for i in range(count)])  20.1 us
    ppermute x11, starting transfers between devices, shift(): lax.ppermute(values, axis, [(i, (i + by) % count) for i in range(count)])  17.5 us
    unnamed x16, local copies, waits for them, and re-layouts  9.72 us
    pallas_call x1, Pallas kernels, shards(): pl.pallas_call(functools.partial(first_kernel, (frames_dev, per_frame, wi...  7.74 us
    pallas_call x1, Pallas kernels, shards(): pl.pallas_call(functools.partial(second_kernel, (frames_dev, per_frame, w...  5.45 us
    all_to_all x1, starting transfers between devices, shards(): blocks = lax.all_to_all(packed, 'col', 0, 0, tiled=True)  5.2 us
    pallas_call x1, Pallas kernels, shards(): pl.pallas_call(functools.partial(third_kernel, (frames_dev, per_frame, wi...  4.9 us
  transfers between devices with their start and end apart: 17, of which 14 were waited for; matrix products, arithmetic and copies ran while one was open for 1% of the time, Pallas kernels for 0%

profile of v1, /device:TPU:0, one launch (start us, length us, event | category | flops | bytes accessed | tf_op | source)
XLA Modules:
  0.0 118.7 jit_solution(227103547414611815)
XLA Ops:
  6.1 1.4 %copy-done.3 = f32[8,200,384]{2,1,0:T(8,128)} copy-done((f32[8,200,384]{2,1,0:T(8,128)}, f32[8,200,384]{2,1,0:T(8,128)S(1)}, u32[]{:S(2)}) %copy-start.3) | copy-done | bytes 2457624
  7.6 5.2 %all-to-all-start = ((f32[8,200,384]{2,1,0:T(8,128)}), f32[8,200,384]{2,1,0:T(8,128)S(1)}, u32[]{:S(2)}, u32[]{:S(2)}) async-start(f32[8,200,384]{2,1,0:T(8,128)} %copy-done.3), calls=%async_computation | async-start | bytes 4915200 | tf_op jit(solution)/shard_map/all_to_all | solution.py:404
  12.9 30.4 %all-to-all-done.tails.block = f32[8,200,384]{2,1,0:T(8,128)S(1)} async-done(((f32[8,200,384]{2,1,0:T(8,128)}), f32[8,200,384]{2,1,0:T(8,128)S(1)}, u32[]{:S(2)}, u32[]{:S(2)}) %all-to-all-start) | async-done | bytes 2457632 | tf_op jit(solution)/shard_map/all_to_all | solution.py:404
  43.3 3.7 %collective-permute-start.1 = (f32[2,16,384]{2,1,0:T(8,128)S(1)}, f32[2,16,384]{2,1,0:T(8,128)S(1)}, u32[]{:S(2)}, u32[]{:S(2)}) collective-permute-start(f32[2,16,384]{2,1,0:T(8,128)S(1)} %gather_table.1.own), channel_id=1, source_target_pairs={{0,24},{8,0},{16,8},{24,16},{1,25},{9,1},{17,9},{25,17},{2,26},{10... | collective-permute-start | bytes 147464 | tf_op jit(solution)/shard_map/ppermute | solution.py:323
  47.0 1.7 %collective-permute-done.1.following = f32[2,16,384]{2,1,0:T(8,128)S(1)} collective-permute-done((f32[2,16,384]{2,1,0:T(8,128)S(1)}, f32[2,16,384]{2,1,0:T(8,128)S(1)}, u32[]{:S(2)}, u32[]{:S(2)}) %collective-permute-start.1) | collective-permute-done | bytes 49184 | tf_op jit(solution)/shard_map/ppermute | solution.py:323
  48.7 4.1 %collective-permute-done.prev = f32[2,16,384]{2,1,0:T(8,128)S(1)} collective-permute-done((f32[2,16,384]{2,1,0:T(8,128)S(1)}, f32[2,16,384]{2,1,0:T(8,128)S(1)}, u32[]{:S(2)}, u32[]{:S(2)}) %collective-permute-start) | collective-permute-done | bytes 49184 | tf_op jit(solution)/shard_map/ppermute | solution.py:323
  52.8 7.7 %first_pass.1 = (f32[2,16,384]{2,1,0:T(8,128)S(1)}, f32[2,16,384]{2,1,0:T(8,128)S(1)}, f32[2,16,384]{2,1,0:T(8,128)S(1)}, f32[8,6,48,384]{3,2,1,0:T(8,128)S(1)}, f32[384,128]{1,0:T(8,128)S(1)}) custom-call(f32[1,48]{1,0:T(1,128)S(1)} %fusion.23.slot_row, f32[48,1]{1,0:T(8,128)S(1)} %fusion.11.slot_col, f32[2,384]{1,0:T(2,128)S(1)} %pad_maximum_fusion.1.rays, ...), custom_call_target="tpu_custom_call" | custom-call | tf_op jit(solution)/shard_map/first_pass/pallas_call | solution.py:433
  60.6 1.7 %copy-done = f32[8,6,48,384]{3,2,1,0:T(8,128)} copy-done((f32[8,6,48,384]{3,2,1,0:T(8,128)}, f32[8,6,48,384]{3,2,1,0:T(8,128)S(1)}, u32[]{:S(2)}) %copy-start) | copy-done | bytes 3538968
  62.3 3.8 %collective-permute-start.3 = (f32[2,16,384]{2,1,0:T(8,128)S(1)}, f32[2,16,384]{2,1,0:T(8,128)S(1)}, u32[]{:S(2)}, u32[]{:S(2)}) collective-permute-start(f32[2,16,384]{2,1,0:T(8,128)S(1)} %get-tuple-element.13), channel_id=1, source_target_pairs={{0,24},{8,0},{16,8},{24,16},{1,25},{9,1},{17,9},{25,17},{2,26},{10... | collective-permute-start | bytes 147464 | tf_op jit(solution)/shard_map/ppermute | solution.py:323
  66.2 2.3 %collective-permute-done.2 = f32[2,16,384]{2,1,0:T(8,128)S(1)} collective-permute-done((f32[2,16,384]{2,1,0:T(8,128)S(1)}, f32[2,16,384]{2,1,0:T(8,128)S(1)}, u32[]{:S(2)}, u32[]{:S(2)}) %collective-permute-start.2) | collective-permute-done | bytes 49184 | tf_op jit(solution)/shard_map/ppermute | solution.py:323
  68.5 4.1 %collective-permute-start.5 = (f32[2,16,384]{2,1,0:T(8,128)S(1)}, f32[2,16,384]{2,1,0:T(8,128)S(1)}, u32[]{:S(2)}, u32[]{:S(2)}) collective-permute-start(f32[2,16,384]{2,1,0:T(8,128)S(1)} %pad_maximum_fusion.own), channel_id=1, source_target_pairs={{0,24},{8,0},{16,8},{24,16},{1,25},{9,1},{17,9},{25,17},{2,26},{10... | collective-permute-start | bytes 147464 | tf_op jit(solution)/shard_map/ppermute | solution.py:323
  72.6 1.7 %collective-permute-done.5.following = f32[2,16,384]{2,1,0:T(8,128)S(1)} collective-permute-done((f32[2,16,384]{2,1,0:T(8,128)S(1)}, f32[2,16,384]{2,1,0:T(8,128)S(1)}, u32[]{:S(2)}, u32[]{:S(2)}) %collective-permute-start.5) | collective-permute-done | bytes 49184 | tf_op jit(solution)/shard_map/ppermute | solution.py:323
  74.4 4.1 %collective-permute-done.4.prev = f32[2,16,384]{2,1,0:T(8,128)S(1)} collective-permute-done((f32[2,16,384]{2,1,0:T(8,128)S(1)}, f32[2,16,384]{2,1,0:T(8,128)S(1)}, u32[]{:S(2)}, u32[]{:S(2)}) %collective-permute-start.4) | collective-permute-done | bytes 49184 | tf_op jit(solution)/shard_map/ppermute | solution.py:323
  78.5 2.0 %copy-done.1 = f32[8,6,48,384]{3,2,1,0:T(8,128)S(1)} copy-done((f32[8,6,48,384]{3,2,1,0:T(8,128)S(1)}, f32[8,6,48,384]{3,2,1,0:T(8,128)}, u32[]{:S(2)}) %copy-start.1) | copy-done | bytes 3538968
  80.5 5.5 %second_pass.1 = f32[32,64]{1,0:T(8,128)S(1)} custom-call(f32[1,48]{1,0:T(1,128)S(1)} %fusion.23.slot_row, s32[1]{0:T(128)} %bitcast.3.first, f32[8,200,384]{2,1,0:T(8,128)S(1)} %all-to-all-done.tails.block, f32[8,6,48,384]{3,2,1,0:T(8,128)S(1)} %copy-done.1, f32[384,128]{1,0:T(8,128)S(1)} %get-tuple-element.15.sums, ...), custom_call_target="tpu_custom_call" | custom-call | tf_op jit(solution)/shard_map/second_pass/pallas_call | solution.py:465
  87.5 2.0 %collective-permute-start.6 = (f32[32,64]{1,0:T(8,128)S(1)}, f32[32,64]{1,0:T(8,128)S(1)}, u32[]{:S(2)}, u32[]{:S(2)}) collective-permute-start(f32[32,64]{1,0:T(8,128)S(1)} %second_pass.1), channel_id=1, source_target_pairs={{0,2},{1,3},{2,0},{3,1},{4,6},{5,7},{6,4},{7,5},{8,10},{9,11},{10,... | collective-permute-start | bytes 24584 | tf_op jit(solution)/shard_map/ppermute | solution.py:334
  92.6 1.8 %collective-permute-start.10 = (f32[32,64]{1,0:T(8,128)S(1)}, f32[32,64]{1,0:T(8,128)S(1)}, u32[]{:S(2)}, u32[]{:S(2)}) collective-permute-start(f32[32,64]{1,0:T(8,128)S(1)} %add.258.refs_0_), channel_id=1, source_target_pairs={{0,8},{8,16},{16,24},{24,0},{1,9},{9,17},{17,25},{25,1},{2,10},{10... | collective-permute-start | bytes 24584 | tf_op jit(solution)/shard_map/ppermute | solution.py:323
  94.5 1.7 %collective-permute-done.12.refs_3_ = f32[32,64]{1,0:T(8,128)S(1)} collective-permute-done((f32[32,64]{1,0:T(8,128)S(1)}, f32[32,64]{1,0:T(8,128)S(1)}, u32[]{:S(2)}, u32[]{:S(2)}) %collective-permute-start.12) | collective-permute-done | bytes 8224 | tf_op jit(solution)/shard_map/ppermute | solution.py:323
  97.1 1.6 %collective-permute-done.10.refs_1_ = f32[32,64]{1,0:T(8,128)S(1)} collective-permute-done((f32[32,64]{1,0:T(8,128)S(1)}, f32[32,64]{1,0:T(8,128)S(1)}, u32[]{:S(2)}, u32[]{:S(2)}) %collective-permute-start.10) | collective-permute-done | bytes 8224 | tf_op jit(solution)/shard_map/ppermute | solution.py:323
  98.7 4.9 %third_pass.1 = (f32[16,384]{1,0:T(8,128)S(1)}, f32[16,384]{1,0:T(8,128)S(1)}, f32[16,384]{1,0:T(8,128)S(1)}, f32[8,64]{1,0:T(8,128)S(1)}) custom-call(f32[48,1]{1,0:T(8,128)S(1)} %fusion.11.slot_col, s32[1]{0:T(128)} %bitcast.3.first, f32[8,200,384]{2,1,0:T(8,128)S(1)} %all-to-all-done.tails.block, f32[8,6,48,384]{3,2,1,0:T(8,128)S(1)} %copy-done.2, ...), custom_call_target="tpu_custom_call" | custom-call | tf_op jit(solution)/shard_map/third_pass/pallas_call | solution.py:483
  104.1 3.4 %collective-permute-start.14 = (f32[16,384]{1,0:T(8,128)S(1)}, f32[16,384]{1,0:T(8,128)S(1)}, u32[]{:S(2)}, u32[]{:S(2)}) collective-permute-start(f32[16,384]{1,0:T(8,128)S(1)} %get-tuple-element.18), channel_id=1, source_target_pairs={{0,24},{8,0},{16,8},{24,16},{1,25},{9,1},{17,9},{25,17},{2,26},{10... | collective-permute-start | bytes 73736 | tf_op jit(solution)/shard_map/ppermute | solution.py:323
  107.5 1.8 %collective-permute-done.13 = f32[16,384]{1,0:T(8,128)S(1)} collective-permute-done((f32[16,384]{1,0:T(8,128)S(1)}, f32[16,384]{1,0:T(8,128)S(1)}, u32[]{:S(2)}, u32[]{:S(2)}) %collective-permute-start.13) | collective-permute-done | bytes 24608 | tf_op jit(solution)/shard_map/ppermute | solution.py:323
  109.9 3.3 %all-to-all-start.1 = ((f32[8,2,384]{2,1,0:T(2,128)}), f32[8,2,384]{2,1,0:T(2,128)S(1)}, u32[]{:S(2)}, u32[]{:S(2)}) async-start(f32[8,2,384]{2,1,0:T(2,128)} %reshape.311), calls=%async_computation.1 | async-start | bytes 49152 | tf_op jit(solution)/shard_map/all_to_all | solution.py:496
  114.0 4.0 %all-to-all-done.1 = f32[8,2,384]{2,1,0:T(2,128)S(1)} async-done(((f32[8,2,384]{2,1,0:T(2,128)}), f32[8,2,384]{2,1,0:T(2,128)S(1)}, u32[]{:S(2)}, u32[]{:S(2)}) %all-to-all-start.1) | async-done | bytes 24608 | tf_op jit(solution)/shard_map/all_to_all | solution.py:496
  (51 shorter events, 13.6 us)
Async XLA Ops:
  2.3 1.3 %copy-start.4 = (f32[2,2,24,3072]{3,2,1,0:T(8,128)S(1)}, f32[2,2,24,3072]{3,2,1,0:T(8,128)}, u32[]{:S(2)}) copy-start(f32[2,2,24,3072]{3,2,1,0:T(8,128)} %flow.1) | copy-start | bytes 3538948
  3.6 1.3 %copy-start.5 = (f32[2,2,24,3072]{3,2,1,0:T(8,128)S(1)}, f32[2,2,24,3072]{3,2,1,0:T(8,128)}, u32[]{:S(2)}) copy-start(f32[2,2,24,3072]{3,2,1,0:T(8,128)} %weight.1) | copy-start | bytes 3538948
  4.9 0.7 copy-start.6
  6.1 1.4 %copy-start.3 = (f32[8,200,384]{2,1,0:T(8,128)}, f32[8,200,384]{2,1,0:T(8,128)S(1)}, u32[]{:S(2)}) copy-start(f32[8,200,384]{2,1,0:T(8,128)S(1)} %pack.1) | copy-start | bytes 7372804
  7.6 35.7 %all-to-all-start = ((f32[8,200,384]{2,1,0:T(8,128)}), f32[8,200,384]{2,1,0:T(8,128)S(1)}, u32[]{:S(2)}, u32[]{:S(2)}) async-start(f32[8,200,384]{2,1,0:T(8,128)} %copy-done.3), calls=%async_computation | async-start | bytes 4915200 | tf_op jit(solution)/shard_map/all_to_all | solution.py:404
  43.3 5.4 %collective-permute-start.1 = (f32[2,16,384]{2,1,0:T(8,128)S(1)}, f32[2,16,384]{2,1,0:T(8,128)S(1)}, u32[]{:S(2)}, u32[]{:S(2)}) collective-permute-start(f32[2,16,384]{2,1,0:T(8,128)S(1)} %gather_table.1.own), channel_id=1, source_target_pairs={{0,24},{8,0},{16,8},{24,16},{1,25},{9,1},{17,9},{25,17},{2,26},{10... | collective-permute-start | bytes 147464 | tf_op jit(solution)/shard_map/ppermute | solution.py:323
  46.9 5.9 %collective-permute-start = (f32[2,16,384]{2,1,0:T(8,128)S(1)}, f32[2,16,384]{2,1,0:T(8,128)S(1)}, u32[]{:S(2)}, u32[]{:S(2)}) collective-permute-start(f32[2,16,384]{2,1,0:T(8,128)S(1)} %gather_table.1.own), channel_id=1, source_target_pairs={{0,8},{8,16},{16,24},{24,0},{1,9},{9,17},{17,25},{25,1},{2,10},{10... | collective-permute-start | bytes 147464 | tf_op jit(solution)/shard_map/ppermute | solution.py:323
  60.6 1.7 %copy-start = (f32[8,6,48,384]{3,2,1,0:T(8,128)}, f32[8,6,48,384]{3,2,1,0:T(8,128)S(1)}, u32[]{:S(2)}) copy-start(f32[8,6,48,384]{3,2,1,0:T(8,128)S(1)} %get-tuple-element.14.maps) | copy-start | bytes 10616836
  62.3 6.2 %collective-permute-start.2 = (f32[2,16,384]{2,1,0:T(8,128)S(1)}, f32[2,16,384]{2,1,0:T(8,128)S(1)}, u32[]{:S(2)}, u32[]{:S(2)}) collective-permute-start(f32[2,16,384]{2,1,0:T(8,128)S(1)} %get-tuple-element.12), channel_id=1, source_target_pairs={{0,8},{8,16},{16,24},{24,0},{1,9},{9,17},{17,25},{25,1},{2,10},{10... | collective-permute-start | bytes 147464 | tf_op jit(solution)/shard_map/ppermute | solution.py:323
  62.3 6.2 %collective-permute-start.3 = (f32[2,16,384]{2,1,0:T(8,128)S(1)}, f32[2,16,384]{2,1,0:T(8,128)S(1)}, u32[]{:S(2)}, u32[]{:S(2)}) collective-permute-start(f32[2,16,384]{2,1,0:T(8,128)S(1)} %get-tuple-element.13), channel_id=1, source_target_pairs={{0,24},{8,0},{16,8},{24,16},{1,25},{9,1},{17,9},{25,17},{2,26},{10... | collective-permute-start | bytes 147464 | tf_op jit(solution)/shard_map/ppermute | solution.py:323
  68.5 5.9 %collective-permute-start.5 = (f32[2,16,384]{2,1,0:T(8,128)S(1)}, f32[2,16,384]{2,1,0:T(8,128)S(1)}, u32[]{:S(2)}, u32[]{:S(2)}) collective-permute-start(f32[2,16,384]{2,1,0:T(8,128)S(1)} %pad_maximum_fusion.own), channel_id=1, source_target_pairs={{0,24},{8,0},{16,8},{24,16},{1,25},{9,1},{17,9},{25,17},{2,26},{10... | collective-permute-start | bytes 147464 | tf_op jit(solution)/shard_map/ppermute | solution.py:323
  72.6 5.9 %collective-permute-start.4 = (f32[2,16,384]{2,1,0:T(8,128)S(1)}, f32[2,16,384]{2,1,0:T(8,128)S(1)}, u32[]{:S(2)}, u32[]{:S(2)}) collective-permute-start(f32[2,16,384]{2,1,0:T(8,128)S(1)} %pad_maximum_fusion.own), channel_id=1, source_target_pairs={{0,8},{8,16},{16,24},{24,0},{1,9},{9,17},{17,25},{25,1},{2,10},{10... | collective-permute-start | bytes 147464 | tf_op jit(solution)/shard_map/ppermute | solution.py:323
  78.5 2.0 %copy-start.1 = (f32[8,6,48,384]{3,2,1,0:T(8,128)S(1)}, f32[8,6,48,384]{3,2,1,0:T(8,128)}, u32[]{:S(2)}) copy-start(f32[8,6,48,384]{3,2,1,0:T(8,128)} %copy-done) | copy-start | bytes 10616836
  80.5 18.2 %copy-start.2 = (f32[8,6,48,384]{3,2,1,0:T(8,128)S(1)}, f32[8,6,48,384]{3,2,1,0:T(8,128)}, u32[]{:S(2)}) copy-start(f32[8,6,48,384]{3,2,1,0:T(8,128)} %copy-done) | copy-start | bytes 10616836
  86.0 4.7 %collective-permute-start.8 = (f32[32,64]{1,0:T(8,128)S(1)}, f32[32,64]{1,0:T(8,128)S(1)}, u32[]{:S(2)}, u32[]{:S(2)}) collective-permute-start(f32[32,64]{1,0:T(8,128)S(1)} %second_pass.1), channel_id=1, source_target_pairs={{0,6},{1,7},{2,4},{3,5},{4,2},{5,3},{6,0},{7,1},{8,14},{9,15},{10,... | collective-permute-start | bytes 24584 | tf_op jit(solution)/shard_map/ppermute | solution.py:334
  86.1 4.5 %collective-permute-start.7 = (f32[32,64]{1,0:T(8,128)S(1)}, f32[32,64]{1,0:T(8,128)S(1)}, u32[]{:S(2)}, u32[]{:S(2)}) collective-permute-start(f32[32,64]{1,0:T(8,128)S(1)} %second_pass.1), channel_id=1, source_target_pairs={{0,4},{1,5},{2,6},{3,7},{4,0},{5,1},{6,2},{7,3},{8,12},{9,13},{10,... | collective-permute-start | bytes 24584 | tf_op jit(solution)/shard_map/ppermute | solution.py:334
  87.5 3.7 %collective-permute-start.6 = (f32[32,64]{1,0:T(8,128)S(1)}, f32[32,64]{1,0:T(8,128)S(1)}, u32[]{:S(2)}, u32[]{:S(2)}) collective-permute-start(f32[32,64]{1,0:T(8,128)S(1)} %second_pass.1), channel_id=1, source_target_pairs={{0,2},{1,3},{2,0},{3,1},{4,6},{5,7},{6,4},{7,5},{8,10},{9,11},{10,... | collective-permute-start | bytes 24584 | tf_op jit(solution)/shard_map/ppermute | solution.py:334
  91.2 1.2 collective-permute-start.9
  92.4 3.8 %collective-permute-start.12 = (f32[32,64]{1,0:T(8,128)S(1)}, f32[32,64]{1,0:T(8,128)S(1)}, u32[]{:S(2)}, u32[]{:S(2)}) collective-permute-start(f32[32,64]{1,0:T(8,128)S(1)} %add.258.refs_0_), channel_id=1, source_target_pairs={{0,24},{8,0},{16,8},{24,16},{1,25},{9,1},{17,9},{25,17},{2,26},{10... | collective-permute-start | bytes 24584 | tf_op jit(solution)/shard_map/ppermute | solution.py:323
  92.4 4.7 %collective-permute-start.11 = (f32[32,64]{1,0:T(8,128)S(1)}, f32[32,64]{1,0:T(8,128)S(1)}, u32[]{:S(2)}, u32[]{:S(2)}) collective-permute-start(f32[32,64]{1,0:T(8,128)S(1)} %add.258.refs_0_), channel_id=1, source_target_pairs={{0,16},{8,24},{16,0},{24,8},{1,17},{9,25},{17,1},{25,9},{2,18},{10... | collective-permute-start | bytes 24584 | tf_op jit(solution)/shard_map/ppermute | solution.py:323
  92.6 6.1 %collective-permute-start.10 = (f32[32,64]{1,0:T(8,128)S(1)}, f32[32,64]{1,0:T(8,128)S(1)}, u32[]{:S(2)}, u32[]{:S(2)}) collective-permute-start(f32[32,64]{1,0:T(8,128)S(1)} %add.258.refs_0_), channel_id=1, source_target_pairs={{0,8},{8,16},{16,24},{24,0},{1,9},{9,17},{17,25},{25,1},{2,10},{10... | collective-permute-start | bytes 24584 | tf_op jit(solution)/shard_map/ppermute | solution.py:323
  103.6 5.7 %collective-permute-start.13 = (f32[16,384]{1,0:T(8,128)S(1)}, f32[16,384]{1,0:T(8,128)S(1)}, u32[]{:S(2)}, u32[]{:S(2)}) collective-permute-start(f32[16,384]{1,0:T(8,128)S(1)} %get-tuple-element.17), channel_id=1, source_target_pairs={{0,8},{8,16},{16,24},{24,0},{1,9},{9,17},{17,25},{25,1},{2,10},{10... | collective-permute-start | bytes 73736 | tf_op jit(solution)/shard_map/ppermute | solution.py:323
  104.1 5.2 %collective-permute-start.14 = (f32[16,384]{1,0:T(8,128)S(1)}, f32[16,384]{1,0:T(8,128)S(1)}, u32[]{:S(2)}, u32[]{:S(2)}) collective-permute-start(f32[16,384]{1,0:T(8,128)S(1)} %get-tuple-element.18), channel_id=1, source_target_pairs={{0,24},{8,0},{16,8},{24,16},{1,25},{9,1},{17,9},{25,17},{2,26},{10... | collective-permute-start | bytes 73736 | tf_op jit(solution)/shard_map/ppermute | solution.py:323
  109.9 8.1 %all-to-all-start.1 = ((f32[8,2,384]{2,1,0:T(2,128)}), f32[8,2,384]{2,1,0:T(2,128)S(1)}, u32[]{:S(2)}, u32[]{:S(2)}) async-start(f32[8,2,384]{2,1,0:T(2,128)} %reshape.311), calls=%async_computation.1 | async-start | bytes 49152 | tf_op jit(solution)/shard_map/all_to_all | solution.py:496

commit v2 on v0

v2 whole, which is shorter than its diff:
```python
import functools

import jax
import jax.numpy as jnp
from jax import lax
from jax.experimental import pallas as pl
from jax.experimental.pallas import tpu as pltpu
from jax.sharding import PartitionSpec as P


IMG_H = 48
IMG_W = 64
DAMP_DEPTH = 0.1
LEVENBERG = 0.1
RIDGE = 0.001
TAIL = 8
LANES = 128
U_AXES = (0, 1, 2, 3, 5)
V_AXES = (0, 1, 2, 4, 5)
PAIRS = [(i, j) for i in range(6) for j in range(i + 1)]
F32 = jnp.float32
BF16 = jnp.bfloat16
VMEM = pl.BlockSpec(memory_space=pltpu.VMEM)
SMEM = pl.BlockSpec(memory_space=pltpu.SMEM)


def call(kernel, ins, outs, scratch=(), specs=None, flops=1_000_000):
    shapes = [jax.ShapeDtypeStruct(*out) for out in outs]
    return pl.pallas_call(
        kernel,
        in_specs=specs or [VMEM] * len(ins),
        out_specs=[VMEM] * len(shapes),
        out_shape=shapes,
        scratch_shapes=list(scratch),
        compiler_params=pltpu.CompilerParams(vmem_limit_bytes=28 * 1024 * 1024),
        cost_estimate=pl.CostEstimate(flops=flops, bytes_accessed=0, transcendentals=0),
    )(*ins)


def split3(x):
    high = x.astype(BF16)
    rest = x - high.astype(F32)
    mid = rest.astype(BF16)
    low = (rest - mid.astype(F32)).astype(BF16)
    return high, mid, low


def stack3(x):
    return jnp.concatenate(split3(x), axis=0)


def dot(a, b, dims=((1,), (0,))):
    return lax.dot_general(a, b, (dims, ((), ())), preferred_element_type=F32)


def dot3(hot, x, dims):
    high, mid, low = split3(x)
    return dot(hot, low, dims) + dot(hot, mid, dims) + dot(hot, high, dims)


DOWN = ((0,), (0,))
ACROSS = ((1,), (1,))


def lane_tiles(width):
    step = LANES if width % LANES == 0 else width
    return [slice(start, start + step) for start in range(0, width, step)]


def as_column(row, count):
    across = lax.broadcasted_iota(jnp.int32, (count, count), 1)
    down = lax.broadcasted_iota(jnp.int32, (count, count), 0)
    return jnp.sum(jnp.where(across == down, row, 0.0), axis=1, keepdims=True)


def local_source(device, shape, per_frame, frames_dev):
    edge = lax.broadcasted_iota(jnp.int32, shape, 0)
    frame = jnp.zeros(shape, jnp.int32)
    for k in range(1, frames_dev):
        frame = frame + (edge >= k * per_frame).astype(jnp.int32)
    return frame + device * frames_dev


def as_hot(test):
    return jnp.where(test, 1.0, 0.0).astype(F32)


def near(offset, rows):
    offset = offset % rows
    return offset if offset <= 1 else offset - rows


def sent_blocks(by, rows):
    return [o for o in (-1, 0, 1) if near(o + by, rows) in (-1, 0, 1)]


def reduce_lanes(partial):
    lane = lax.broadcasted_iota(jnp.int32, (8, LANES), 1)
    packed = jnp.zeros((8, LANES), F32)
    for k in sorted(partial):
        packed = jnp.where(lane == k, jnp.sum(partial[k], axis=1, keepdims=True), packed)
    return packed


class Sums(dict):
    def put(self, key, value):
        self[key] = value if key not in self else self[key] + value


def copy_kernel(count, *refs):
    for k in range(count):
        refs[1 + count + k][...] = refs[1 + k][...]


def cut_for_chips(values, chip, chips, axis_of):
    width = values.shape[2] // chips
    ids = jnp.stack([axis_of(chip, s) for s in range(chips)]).astype(jnp.int32)
    if width % LANES:
        return [
            lax.dynamic_slice_in_dim(values, ids[s] * width, width, axis=2) for s in range(chips)
        ]
    shape = values.shape[:2] + (width,)
    return pl.pallas_call(
        functools.partial(copy_kernel, chips),
        grid_spec=pltpu.PrefetchScalarGridSpec(
            num_scalar_prefetch=1,
            grid=(1,),
            in_specs=[
                pl.BlockSpec(shape, lambda i, ids, s=s: (0, 0, ids[s])) for s in range(chips)
            ],
            out_specs=[pl.BlockSpec(shape, lambda i, ids: (0, 0, 0))] * chips,
        ),
        out_shape=[jax.ShapeDtypeStruct(shape, F32)] * chips,
        compiler_params=pltpu.CompilerParams(vmem_limit_bytes=28 * 1024 * 1024),
        name="cut",
    )(ids, *([values] * chips))


def mark_kernel(source, out):
    out[...] = source[0:8, :] + 1.0


def mark(values):
    (out,) = call(mark_kernel, [values], [((8, values.shape[1]), F32)], flops=100)
    return out


def halve_kernel(width, core, *refs):
    refs = refs[1:]
    count = len(refs) - 2
    keep, send = refs[count:]
    mine = pl.multiple_of(core[0] * width, LANES)
    other = pl.multiple_of((1 - core[0]) * width, LANES)
    for s in range(count):
        rows = refs[s].shape[1]
        keep[:, s * rows : (s + 1) * rows, :] = refs[s][:, :, pl.ds(mine, width)]
        send[:, s * rows : (s + 1) * rows, :] = refs[s][:, :, pl.ds(other, width)]


def halve(parts, core, after):
    width = parts[0].shape[2] // 2
    if width % LANES:
        whole = jnp.concatenate(lax.optimization_barrier((*parts, after))[:-1], axis=1)
        return [
            lax.dynamic_slice_in_dim(whole, start * width, width, axis=2) for start in (core, 1 - core)
        ]
    shape = (parts[0].shape[0], len(parts) * parts[0].shape[1], width)
    return call(
        functools.partial(halve_kernel, width),
        [core.astype(jnp.int32).reshape(1), after, *parts],
        [(shape, F32)] * 2,
        specs=[SMEM] + [VMEM] * (len(parts) + 1),
    )


def table_kernel(dims, devices, first, ids, slot_at, tails, tails_other, table, hot, pair, plus, minus):
    frames_dev, per_frame, _, group, frames = dims
    edges = frames_dev * per_frame
    chips = tails.shape[1] // TAIL
    wide = ids.shape[1]
    for h, ref in enumerate((tails, tails_other)):
        for s in range(chips):
            j = h * chips + s
            dev = devices[j]
            for f in range(frames_dev):
                row = dev * frames_dev + f
                table[0, pl.ds(row, 1), :] = ref[0, s * TAIL + f : s * TAIL + f + 1, :]
                at = s * TAIL + frames_dev + f
                table[1, pl.ds(row, 1), :] = ref[0, at : at + 1, :]
            at = s * TAIL + 2 * frames_dev
            column = as_column(ref[0, at : at + 1, 0:edges], edges)
            here = slice(j * edges, (j + 1) * edges)
            target = as_hot(column == ids[...])
            local = local_source(dev, (edges, wide), per_frame, frames_dev)
            hot[here, :] = target.astype(BF16)
            pair[here, :] = (as_hot(slot_at[...] == local + group) - target).astype(BF16)
            frame = lax.broadcasted_iota(jnp.int32, (edges, frames), 1)
            source = as_hot(frame == local_source(dev, (edges, frames), per_frame, frames_dev) + first[0])
            target = as_hot(frame.astype(F32) == column)
            plus[here, :] = (source + target).astype(BF16)
            minus[here, :] = (source - target).astype(BF16)


def geometry(rel, rays, lanes, dep):
    w0, w1, w2, m0, m1, m2 = [rel[:, i : i + 1] for i in range(6)]
    x = rays[0:1, lanes]
    y = rays[1:2, lanes]
    x0 = x + w1 - w2 * y + m0 * dep
    x1 = y + w2 * x - w0 + m1 * dep
    x2 = 1.0 + w0 * y - w1 * x + m2 * dep
    q = 1.0 / x2
    u = x0 * q
    v = x1 * q
    dq = dep * q
    uq = u * q
    vq = v * q
    ju = {0: -y * uq, 1: q + x * uq, 2: -y * q, 3: dq, 5: -u * dq}
    jv = {0: -q - y * vq, 1: x * vq, 2: x * q, 4: dq, 5: -v * dq}
    du = q * (m0 - u * m2)
    dv = q * (m1 - v * m2)
    return u - x, v - y, du, dv, ju, jv


def for_groups(count, body, unroll=2):
    lax.fori_loop(0, count, lambda g, carry: (body(g), carry)[1], 0, unroll=unroll)


def weight_kernel(dims, rays, keep, got, own, prev, following, hot, pair, *refs):
    _, rows, width = dims
    sends = refs[: rows - 1]
    stay, maps, slopes, lean_u, lean_v, sums, depth_e, rel_e, curv = refs[rows - 1 :]
    half = keep.shape[1]
    table = [jnp.concatenate([ref[i] for ref in (prev, own, following)], axis=0) for i in range(2)]
    depth_e[...] = dot(hot[...], stack3(table[0]))
    rel_e[...] = dot(pair[...], stack3(table[1][:, 0 : rel_e.shape[1]]))

    for h, ref in enumerate((keep, got)):

        def body(g, h=h, ref=ref):
            at = pl.ds(pl.multiple_of(g * 8, 8), 8)
            to = pl.ds(pl.multiple_of(h * half + g * 8, 8), 8)
            rel = rel_e[to, :]
            partial = Sums()
            for lanes in lane_tiles(width):
                pu, pv, du, dv, ju, jv = geometry(rel, rays, lanes, depth_e[to, lanes])
                cu = ref[0, at, lanes]
                cv = ref[1, at, lanes]
                cud = cu * du
                cvd = cv * dv
                curv[to, lanes] = cud * du + cvd * dv
                for k, value in enumerate((cud, cvd, pu, pv)):
                    slopes[k, to, lanes] = value
                for a in range(6):
                    terms = [cud * ju[a]] if a in ju else []
                    if a in jv:
                        terms.append(cvd * jv[a])
                    maps[a, to, lanes] = sum(terms[1:], terms[0])
                su = {a: cu * ju[a] for a in ju}
                sv = {a: cv * jv[a] for a in jv}
                for k, (a, c) in enumerate(zip(ju, jv)):
                    lean_u[k, to, lanes] = su[a]
                    lean_v[k, to, lanes] = sv[c]
                for k, (a, b) in enumerate(PAIRS):
                    if a in ju and b in ju:
                        partial.put(k, su[a] * ju[b])
                    if a in jv and b in jv:
                        partial.put(k, sv[a] * jv[b])
            sums[to, :] = reduce_lanes(partial)

        for_groups(half // 8, body)
    scatter(dims, hot, curv[...], sends, stay)


def scatter(dims, hot, values, sends, stay):
    group, rows, _ = dims
    total = dot3(hot[:, 0 : 3 * group], values, DOWN)
    stay[...] = total
    for by, ref in enumerate(sends, 1):
        for k, o in enumerate(sent_blocks(by, rows)):
            ref[k * group : (k + 1) * group, :] = total[(o + 1) * group : (o + 2) * group, :]


def gathered(dims, stay, arrived):
    group, rows, _ = dims
    blocks = [stay[o * group : (o + 1) * group, :] for o in range(3)]
    for by, ref in enumerate(arrived, 1):
        for k, o in enumerate(sent_blocks(by, rows)):
            to = near(o + by, rows) + 1
            blocks[to] = blocks[to] + ref[k * group : (k + 1) * group, :]
    return jnp.concatenate(blocks, axis=0)


def flow_kernel(dims, keep, got, slopes, hot, *refs):
    _, rows, _ = dims
    sends = refs[: rows - 1]
    stay = refs[rows - 1]
    half = keep.shape[1]
    values = []
    for h, ref in enumerate((keep, got)):
        at = slice(h * half, (h + 1) * half)
        ru = ref[0] - slopes[2, at, :]
        rv = ref[1] - slopes[3, at, :]
        values.append(slopes[0, at, :] * ru + slopes[1, at, :] * rv)
    scatter(dims, hot, jnp.concatenate(values, axis=0), sends, stay)


def gradient_kernel(dims, slopes, lean_u, lean_v, flows, flows_got, sums):
    _, _, width = dims
    half = flows.shape[1]
    for h, obs in enumerate((flows, flows_got)):

        def body(g, h=h, obs=obs):
            at = pl.ds(pl.multiple_of(g * 8, 8), 8)
            to = pl.ds(pl.multiple_of(h * half + g * 8, 8), 8)
            partial = Sums()
            for lanes in lane_tiles(width):
                ru = obs[0, at, lanes] - slopes[2, to, lanes]
                rv = obs[1, at, lanes] - slopes[3, to, lanes]
                for k in range(5):
                    partial.put(21 + U_AXES[k], lean_u[k, to, lanes] * ru)
                    partial.put(21 + V_AXES[k], lean_v[k, to, lanes] * rv)
            sums[to, :] = reduce_lanes(partial)

        for_groups(half // 8, body, 4)


def curvature_kernel(dims, maps, sums, hot, plus, *refs):
    _, rows, width = dims
    stay, arrived = refs[0], refs[1:rows]
    inverse, table, inverse_e, edge_rows = refs[rows:]
    inv = 1.0 / (DAMP_DEPTH + gathered(dims, stay, arrived))
    inverse[...] = inv
    inverse_e[...] = dot(hot[...], stack3(inv))

    def body(g):
        to = pl.ds(pl.multiple_of(g * 8, 8), 8)
        partial = Sums()
        for lanes in lane_tiles(width):
            e = [maps[a, to, lanes] for a in range(6)]
            scaled = [value * inverse_e[to, lanes] for value in e]
            for k, (a, b) in enumerate(PAIRS):
                partial.put(k, scaled[a] * e[b])
        edge_rows[to, :] = sums[to, :] - reduce_lanes(partial)

    for_groups(maps.shape[1] // 8, body, 4)
    table[...] = dot3(plus[...], edge_rows[...], DOWN).T[0:32, :]


def schur_kernel(dims, maps, sums, hot, minus, inverse, square, *refs):
    group, rows, width = dims
    stay, arrived = refs[0], refs[1:rows]
    table, keep, scaled_e, edge_rows = refs[rows:]
    grad = gathered(dims, stay, arrived)
    keep[0] = grad[group : 2 * group, :]
    keep[1] = inverse[group : 2 * group, :]
    scaled_e[...] = dot(hot[...], stack3(grad * inverse[...]))

    def body(g):
        to = pl.ds(pl.multiple_of(g * 8, 8), 8)
        partial = Sums()
        for lanes in lane_tiles(width):
            sca = scaled_e[to, lanes]
            for a in range(6):
                partial.put(21 + a, maps[a, to, lanes] * sca)
        edge_rows[to, :] = sums[to, :] - reduce_lanes(partial)

    for_groups(maps.shape[1] // 8, body, 4)
    table[...] = square[...] + dot3(minus[...], edge_rows[...], DOWN).T[0:32, :]


def add_kernel(*refs):
    total = refs[0][...]
    for ref in refs[1:-1]:
        total = total + ref[...]
    refs[-1][...] = total


def solve_rows(entry):
    factor = {}
    scale = {}
    for i in range(6):
        for j in range(i + 1):
            element = entry(PAIRS.index((i, j)))
            if i == j:
                element = element * (1.0 + LEVENBERG) + RIDGE
            for k in range(j):
                element = element - factor[i, k] * factor[j, k]
            if i == j:
                factor[i, j] = jnp.sqrt(element)
                scale[i] = 1.0 / factor[i, j]
            else:
                factor[i, j] = element * scale[j]
    forward = []
    for i in range(6):
        element = entry(21 + i)
        for k in range(i):
            element = element - factor[i, k] * forward[k]
        forward.append(element * scale[i])
    result = [None] * 6
    for i in reversed(range(6)):
        element = forward[i]
        for k in range(i + 1, 6):
            element = element - factor[k, i] * result[k]
        result[i] = element * scale[i]
    return result


def solve_kernel(dims, maps, hot, minus, *refs):
    group, rows, width = dims
    tables = refs[:rows]
    z_prev, z_own, z_next, step_out, motion_e, fix = refs[rows:]
    total = tables[0][...]
    for ref in tables[1:]:
        total = total + ref[...]
    result = solve_rows(lambda k: total[k : k + 1, :])
    steps = jnp.concatenate(result + [jnp.zeros((2, total.shape[1]), F32)], axis=0)
    step_out[...] = steps
    motion_e[...] = dot3(minus[...], steps, ACROSS)

    def body(g):
        to = pl.ds(pl.multiple_of(g * 8, 8), 8)
        motion = motion_e[to, :]
        move = [motion[:, a : a + 1] for a in range(6)]
        for lanes in lane_tiles(width):
            value = maps[0, to, lanes] * move[0]
            for a in range(1, 6):
                value = value + maps[a, to, lanes] * move[a]
            fix[to, lanes] = value

    for_groups(maps.shape[1] // 8, body, 4)
    total = dot3(hot[:, 0 : 3 * group], fix[...], DOWN)
    z_prev[...] = total[0:group, :]
    z_own[...] = total[group : 2 * group, :]
    z_next[...] = total[2 * group : 3 * group, :]


def update_kernel(table, keep, z_own, from_prev, from_next, out):
    out[...] = table[0] + (keep[0] - (z_own[...] + from_prev[...] + from_next[...])) * keep[1]


def sort_kernel(frames_dev, core, table, keep, z_own, from_prev, from_next, stay, send, chunk):
    chunk[...] = table[0] + (keep[0] - (z_own[...] + from_prev[...] + from_next[...])) * keep[1]
    mine = core[0] * frames_dev
    other = (1 - core[0]) * frames_dev
    for chip in range(chunk.shape[0] // (2 * frames_dev)):
        base = chip * 2 * frames_dev
        for f in range(frames_dev):
            row = chip * frames_dev + f
            stay[row : row + 1, :] = chunk[pl.ds(base + mine + f, 1), :]
            send[row : row + 1, :] = chunk[pl.ds(base + other + f, 1), :]


def join_kernel(frames_dev, width, core, ids, stay, got, *outs):
    mine = pl.multiple_of(core[0] * width, LANES)
    other = pl.multiple_of((1 - core[0]) * width, LANES)
    for s, out in enumerate(outs):
        for f in range(frames_dev):
            row = ids[s] * frames_dev + f
            out[f : f + 1, pl.ds(mine, width)] = stay[pl.ds(row, 1), :]
            out[f : f + 1, pl.ds(other, width)] = got[pl.ds(row, 1), :]


def lay_kernel(ids, *refs):
    out = refs[-1]
    for s, ref in enumerate(refs[:-1]):
        width = ref.shape[1]
        out[:, pl.ds(pl.multiple_of(ids[s] * width, LANES), width)] = ref[...]


def shift(values, axis, by):
    count = lax.axis_size(axis)
    return lax.ppermute(values, axis, [(i, (i + by) % count) for i in range(count)])


def other_chip(chip, step, chips):
    return chip ^ step if chips & (chips - 1) == 0 else (step - chip) % chips


def chip_partner(values, step):
    count = lax.axis_size("col")
    chips = count // 2
    pairs = [(i, other_chip(i // 2, step, chips) * 2 + i % 2) for i in range(count)]
    return lax.ppermute(values, "col", pairs)


def core_partner(values):
    count = lax.axis_size("col")
    return lax.ppermute(values, "col", [(i, i ^ 1) for i in range(count)])


def across_chips(parts):
    out = [parts[0]]
    for s, part in enumerate(parts[1:], 1):
        out.append(chip_partner(part, s))
    return out


def shards(inv_depth, rotation, translation, edge_target, flow_obs, weight):
    frames_dev, pixels = inv_depth.shape
    per_frame = edge_target.shape[1]
    edges = frames_dev * per_frame
    columns = lax.axis_size("col")
    chips = columns // 2
    rows = lax.axis_size("row")
    group = frames_dev * columns
    frames = group * rows
    slots = 3 * group
    width = pixels // columns
    total = columns * edges
    my_row = lax.axis_index("row")
    my_col = lax.axis_index("col")
    chip = my_col // 2
    core = my_col % 2
    core_id = core.astype(jnp.int32).reshape(1)
    first = (my_row * group).astype(jnp.int32).reshape(1)
    other = functools.partial(other_chip, chips=chips)
    chip_ids = jnp.stack([other(chip, s) for s in range(chips)]).astype(jnp.int32)
    devices = jnp.concatenate([chip_ids * 2 + core, chip_ids * 2 + (1 - core)]).astype(jnp.int32)

    slot = jnp.arange(slots, dtype=jnp.int32)
    slot_id = ((my_row - 1 + slot // group + rows) % rows) * group + slot % group
    ids3 = jnp.tile(slot_id.astype(F32), 3).reshape(1, 3 * slots)
    slot3 = jnp.tile(slot, 3).reshape(1, 3 * slots)
    index = my_col * width + jnp.arange(width, dtype=jnp.int32)
    across = (index % IMG_W).astype(F32)
    downward = (index // IMG_W).astype(F32)
    rays = jnp.stack([(across + 0.5) / IMG_W - 0.5, (downward + 0.5 - 0.5 * IMG_H) / IMG_W])

    pose = jnp.concatenate([rotation, translation], 0).T
    aux = jnp.concatenate(
        [
            jnp.pad(pose, ((0, 0), (0, width - 6))),
            jnp.pad(edge_target.astype(F32).reshape(1, edges), ((0, 0), (0, width - edges))),
            jnp.zeros((TAIL - 2 * frames_dev - 1, width), F32),
        ],
        0,
    )
    tails = jnp.concatenate([inv_depth, jnp.tile(aux, (1, columns))], 0)

    weight_parts = cut_for_chips(weight.reshape(2, edges, pixels), chip, chips, other)
    tail_parts = cut_for_chips(tails.reshape(1, TAIL, pixels), chip, chips, other)
    flow_parts = cut_for_chips(flow_obs.reshape(2, edges, pixels), chip, chips, other)
    weight_parts = across_chips(weight_parts)
    tail_parts = across_chips(tail_parts)
    flow_parts = across_chips(flow_parts)

    tail_keep, tail_send = halve(tail_parts, core, rays)
    tail_got = core_partner(tail_send)
    own_table, hot, pair, plus, minus = call(
        functools.partial(table_kernel, (frames_dev, per_frame, width, group, frames)),
        [devices, first, ids3, slot3, tail_keep, tail_got],
        [
            ((2, group, width), F32),
            ((total, 3 * slots), BF16),
            ((total, 3 * slots), BF16),
            ((total, frames), BF16),
            ((total, frames), BF16),
        ],
        specs=[SMEM, SMEM, VMEM, VMEM, VMEM, VMEM],
    )
    prev_table = shift(own_table, "row", 1)
    next_table = shift(own_table, "row", -1)

    weight_keep, weight_send = halve(weight_parts, core, mark(own_table[0]))
    weight_got = core_partner(weight_send)
    dims = (group, rows, width)
    send_shapes = [
        ((len(sent_blocks(by, rows)) * group, width), F32) for by in range(1, rows)
    ]
    rel_width = min(width, LANES)
    outs = call(
        functools.partial(weight_kernel, dims),
        [rays, weight_keep, weight_got, own_table, prev_table, next_table, hot, pair],
        send_shapes
        + [
            ((slots, width), F32),
            ((6, total, width), F32),
            ((4, total, width), F32),
            ((5, total, width), F32),
            ((5, total, width), F32),
            ((total, LANES), F32),
        ],
        scratch=[
            pltpu.VMEM((total, width), F32),
            pltpu.VMEM((total, rel_width), F32),
            pltpu.VMEM((total, width), F32),
        ],
    )
    curv_sends = outs[: rows - 1]
    curv_stay, maps, slopes, lean_u, lean_v, sums = outs[rows - 1 :]
    curv_got = []
    for by, part in enumerate(curv_sends, 1):
        curv_got.append(shift(part, "row", -by))
    inverse, square = call(
        functools.partial(curvature_kernel, dims),
        [maps, sums, hot, plus, curv_stay, *curv_got],
        [((slots, width), F32), ((32, frames), F32)],
        scratch=[pltpu.VMEM((total, width), F32), pltpu.VMEM((total, LANES), F32)],
    )

    flow_keep, flow_send = halve(flow_parts, core, mark(curv_stay))
    flow_got = core_partner(flow_send)
    outs = call(
        functools.partial(flow_kernel, dims),
        [flow_keep, flow_got, slopes, hot],
        send_shapes + [((slots, width), F32)],
    )
    grad_sends, grad_stay = outs[: rows - 1], outs[rows - 1]
    grad_got = []
    for by, part in enumerate(grad_sends, 1):
        grad_got.append(shift(part, "row", -by))
    (grad_sums,) = call(
        functools.partial(gradient_kernel, dims),
        [slopes, lean_u, lean_v, flow_keep, flow_got],
        [((total, LANES), F32)],
    )
    table, kept = call(
        functools.partial(schur_kernel, dims),
        [maps, grad_sums, hot, minus, inverse, square, grad_stay, *grad_got],
        [((32, frames), F32), ((2, group, width), F32)],
        scratch=[pltpu.VMEM((total, width), F32), pltpu.VMEM((total, LANES), F32)],
    )

    arrived = [chip_partner(table, step) for step in range(1, chips)]
    (table,) = call(add_kernel, [table, *arrived], [((32, frames), F32)])
    (table,) = call(add_kernel, [table, core_partner(table)], [((32, frames), F32)])
    tables = [table] + [shift(table, "row", by) for by in range(1, rows)]
    z_prev, z_own, z_next, step = call(
        functools.partial(solve_kernel, dims),
        [maps, hot, minus, *tables],
        [((group, width), F32)] * 3 + [((8, frames), F32)],
        scratch=[pltpu.VMEM((total, 8), F32), pltpu.VMEM((total, width), F32)],
    )
    from_prev = shift(z_next, "row", 1)
    from_next = shift(z_prev, "row", -1)
    ends = [own_table, kept, z_own, from_prev, from_next]
    if width % LANES:
        (chunk,) = call(update_kernel, ends, [((group, width), F32)])
        back = lax.all_to_all(chunk.reshape(columns, frames_dev, width), "col", 0, 0, tiled=True)
        depth_next = back.transpose(1, 0, 2).reshape(frames_dev, pixels)
    else:
        stay, send = call(
            functools.partial(sort_kernel, frames_dev),
            [core_id, *ends],
            [((group // 2, width), F32)] * 2,
            scratch=[pltpu.VMEM((group, width), F32)],
            specs=[SMEM] + [VMEM] * 5,
        )
        got = core_partner(send)
        joined = call(
            functools.partial(join_kernel, frames_dev, width),
            [core_id, chip_ids, stay, got],
            [((frames_dev, 2 * width), F32)] * chips,
            specs=[SMEM, SMEM, VMEM, VMEM],
        )
        (depth_next,) = call(
            lay_kernel,
            [chip_ids, *across_chips(joined)],
            [((frames_dev, pixels), F32)],
            specs=[SMEM] + [VMEM] * chips,
        )
    first_own = (my_row * columns + my_col) * frames_dev
    pose_step = lax.dynamic_slice(step, (0, first_own), (6, frames_dev))
    return depth_next, pose_step


def solution(mesh):
    return jax.shard_map(
        shards,
        mesh=mesh,
        in_specs=(
            P(("row", "col"), None),
            P(None, ("row", "col")),
            P(None, ("row", "col")),
            P(("row", "col"), None),
            P(None, ("row", "col"), None, None),
            P(None, ("row", "col"), None, None),
        ),
        out_specs=(P(("row", "col"), None), P(None, ("row", "col"))),
        check_vma=False,
    )
```

time: 461 us -> 92.9 us (0.20); the launches traced: 454 us -> 92.8 us
  blocking collectives: 130 us -> 0 us
  waiting for transfers between devices: 133 us -> 27.5 us
  matrix products: 101 us -> 0 us
  other arithmetic: 33.8 us -> 0.39 us
  starting transfers between devices: 14.1 us -> 41.4 us
  local copies, waits for them, and re-layouts: 27.4 us -> 2.38 us
  Pallas kernels: 0 us -> 20.1 us
  between operations: 15.2 us -> 0.98 us
    unnamed x5 -> x0, waiting for transfers between devices: 105 us -> none
    dot_general x13 -> x0, matrix products: 101 us -> none  [the longest x1 18.3 us: edge_terms(): jnp.einsum('aep,bep->eab', scaled_v, jac_v, precision=PRECISE)]
    all_gather x3 -> x0, blocking collectives: 89.8 us -> none  [the longest x1 42.3 us: shards(): lax.all_gather(rotation, ('row', 'col'), axis=1, tiled=True)]
    psum x1 -> x0, blocking collectives: 39.9 us -> none  [shards(): block_table = lax.psum(block_table, ('row', 'col'))]
    ppermute x8 -> x33, starting transfers between devices: 13.9 us -> 41.4 us  [the longest x15 21.4 us: chip_partner(): return lax.ppermute(values, 'col', pairs)]
    pallas_call x0 -> x20, Pallas kernels: none -> 20.1 us  [the longest x17 18.3 us: call(): pl.pallas_call(kernel, in_specs=specs or [VMEM] * len(ins), out_specs=[VM...]
    all_gather x1 -> x0, waiting for transfers between devices: 15.4 us -> none  [spread(): return lax.all_gather(nearby, 'col', axis=1, tiled=True)]
    ppermute x8 -> x33, waiting for transfers between devices: 12.6 us -> 27.5 us  [the longest x13 13 us: shift(): lax.ppermute(values, axis, [(i, (i + by) % count) for i in range(count)])]
  transfers between devices with their start and end apart: 11 -> 33, of which waited for: 9 -> 18; matrix products, arithmetic and copies ran while one was open for 5% -> 2% of each run, Pallas kernels for 0% -> 15%
where the time goes in v2:
time: 92.9 us; the launch traced here: 92.8 us
  starting transfers between devices  41.4 us (45%)
  waiting for transfers between devices  27.5 us (30%)
  Pallas kernels  20.1 us (22%)
  local copies, waits for them, and re-layouts  2.38 us (3%)
  between operations  0.98 us (1%)
    ppermute x15, starting transfers between devices, chip_partner(): return lax.ppermute(values, 'col', pairs)  21.4 us
    ppermute x13, starting transfers between devices, shift(): lax.ppermute(values, axis, [(i, (i + by) % count) for i in range(count)])  19.7 us
    pallas_call x17, Pallas kernels, call(): pl.pallas_call(kernel, in_specs=specs or [VMEM] * len(ins), out_specs=[VM...  18.3 us
    ppermute x13, waiting for transfers between devices, shift(): lax.ppermute(values, axis, [(i, (i + by) % count) for i in range(count)])  13 us
    ppermute x15, waiting for transfers between devices, chip_partner(): return lax.ppermute(values, 'col', pairs)  11.2 us
    ppermute x5, waiting for transfers between devices, core_partner(): return lax.ppermute(values, 'col', [(i, i ^ 1) for i in range(count)])  3.3 us
    unnamed x15, local copies, waits for them, and re-layouts  1.97 us
  transfers between devices with their start and end apart: 33, of which 18 were waited for; matrix products, arithmetic and copies ran while one was open for 2% of the time, Pallas kernels for 15%

profile of v2, /device:TPU:0, one launch (start us, length us, event | category | flops | bytes accessed | tf_op | source)
XLA Modules:
  0.0 92.8 jit_solution(256705115968083451)
XLA Ops:
  2.7 3.0 %collective-permute-start.4 = (f32[2,48,768]{2,1,0:T(8,128)S(1)}, f32[2,48,768]{2,1,0:T(8,128)S(1)}, u32[]{:S(2)}, u32[]{:S(2)}) collective-permute-start(f32[2,48,768]{2,1,0:T(8,128)S(1)} %get-tuple-element.60), channel_id=1, source_target_pairs={{0,2},{1,3},{2,0},{3,1},{4,6},{5,7},{6,4},{7,5},{8,10},{9,11},{10,... | collective-permute-start | bytes 884744 | tf_op jit(solution)/shard_map/ppermute | solution.py:483
  8.8 2.9 %collective-permute-start.2 = (f32[1,8,768]{2,1,0:T(8,128)S(1)}, f32[1,8,768]{2,1,0:T(8,128)S(1)}, u32[]{:S(2)}, u32[]{:S(2)}) collective-permute-start(f32[1,8,768]{2,1,0:T(8,128)S(1)} %get-tuple-element.55), channel_id=1, source_target_pairs={{0,6},{1,7},{2,4},{3,5},{4,2},{5,3},{6,0},{7,1},{8,14},{9,15},{10,... | collective-permute-start | bytes 73736 | tf_op jit(solution)/shard_map/ppermute | solution.py:483
  11.8 1.7 %collective-permute-done.refs_2_ = f32[1,8,768]{2,1,0:T(8,128)S(1)} collective-permute-done((f32[1,8,768]{2,1,0:T(8,128)S(1)}, f32[1,8,768]{2,1,0:T(8,128)S(1)}, u32[]{:S(2)}, u32[]{:S(2)}) %collective-permute-start) | collective-permute-done | bytes 24608 | tf_op jit(solution)/shard_map/ppermute | solution.py:483
  13.5 2.7 %collective-permute-start.6 = (f32[2,48,768]{2,1,0:T(8,128)S(1)}, f32[2,48,768]{2,1,0:T(8,128)S(1)}, u32[]{:S(2)}, u32[]{:S(2)}) collective-permute-start(f32[2,48,768]{2,1,0:T(8,128)S(1)} %get-tuple-element.62), channel_id=1, source_target_pairs={{0,6},{1,7},{2,4},{3,5},{4,2},{5,3},{6,0},{7,1},{8,14},{9,15},{10,... | collective-permute-start | bytes 884744 | tf_op jit(solution)/shard_map/ppermute | solution.py:483
  18.3 4.0 %collective-permute-done.6.refs_4_ = f32[2,48,768]{2,1,0:T(8,128)S(1)} collective-permute-done((f32[2,48,768]{2,1,0:T(8,128)S(1)}, f32[2,48,768]{2,1,0:T(8,128)S(1)}, u32[]{:S(2)}, u32[]{:S(2)}) %collective-permute-start.6) | collective-permute-done | bytes 294944 | tf_op jit(solution)/shard_map/ppermute | solution.py:483
  23.1 1.5 %collective-permute-start.10 = (f32[2,48,768]{2,1,0:T(8,128)S(1)}, f32[2,48,768]{2,1,0:T(8,128)S(1)}, u32[]{:S(2)}, u32[]{:S(2)}) collective-permute-start(f32[2,48,768]{2,1,0:T(8,128)S(1)} %get-tuple-element.73), channel_id=1, source_target_pairs={{0,2},{1,3},{2,0},{3,1},{4,6},{5,7},{6,4},{7,5},{8,10},{9,11},{10,... | collective-permute-start | bytes 884744 | tf_op jit(solution)/shard_map/ppermute | solution.py:483
  24.6 1.5 %collective-permute-start.11 = (f32[2,48,768]{2,1,0:T(8,128)S(1)}, f32[2,48,768]{2,1,0:T(8,128)S(1)}, u32[]{:S(2)}, u32[]{:S(2)}) collective-permute-start(f32[2,48,768]{2,1,0:T(8,128)S(1)} %get-tuple-element.74), channel_id=1, source_target_pairs={{0,4},{1,5},{2,6},{3,7},{4,0},{5,1},{6,2},{7,3},{8,12},{9,13},{10,... | collective-permute-start | bytes 884744 | tf_op jit(solution)/shard_map/ppermute | solution.py:483
  26.7 1.5 %collective-permute-start.8 = (f32[2,16,384]{2,1,0:T(8,128)S(1)}, f32[2,16,384]{2,1,0:T(8,128)S(1)}, u32[]{:S(2)}, u32[]{:S(2)}) collective-permute-start(f32[2,16,384]{2,1,0:T(8,128)S(1)} %get-tuple-element.58.own.table), channel_id=1, source_target_pairs={{0,8},{8,16},{16,24},{24,0},{1,9},{9,17},{17,25},{25,1},{2,10},{10... | collective-permute-start | bytes 147464 | tf_op jit(solution)/shard_map/ppermute | solution.py:472
  28.2 4.3 %collective-permute-done.8.prev = f32[2,16,384]{2,1,0:T(8,128)S(1)} collective-permute-done((f32[2,16,384]{2,1,0:T(8,128)S(1)}, f32[2,16,384]{2,1,0:T(8,128)S(1)}, u32[]{:S(2)}, u32[]{:S(2)}) %collective-permute-start.8) | collective-permute-done | bytes 49184 | tf_op jit(solution)/shard_map/ppermute | solution.py:472
  32.6 1.8 %collective-permute-start.9 = (f32[2,16,384]{2,1,0:T(8,128)S(1)}, f32[2,16,384]{2,1,0:T(8,128)S(1)}, u32[]{:S(2)}, u32[]{:S(2)}) collective-permute-start(f32[2,16,384]{2,1,0:T(8,128)S(1)} %get-tuple-element.58.own.table), channel_id=1, source_target_pairs={{0,24},{8,0},{16,8},{24,16},{1,25},{9,1},{17,9},{25,17},{2,26},{10... | collective-permute-start | bytes 147464 | tf_op jit(solution)/shard_map/ppermute | solution.py:472
  34.3 2.3 %collective-permute-done.9.following = f32[2,16,384]{2,1,0:T(8,128)S(1)} collective-permute-done((f32[2,16,384]{2,1,0:T(8,128)S(1)}, f32[2,16,384]{2,1,0:T(8,128)S(1)}, u32[]{:S(2)}, u32[]{:S(2)}) %collective-permute-start.9) | collective-permute-done | bytes 49184 | tf_op jit(solution)/shard_map/ppermute | solution.py:472
  36.7 7.1 %shard_map.81 = (f32[32,384]{1,0:T(8,128)S(1)}, f32[32,384]{1,0:T(8,128)S(1)}, f32[32,384]{1,0:T(8,128)S(1)}, f32[48,384]{1,0:T(8,128)S(1)}, f32[6,384,384]{2,1,...) custom-call(f32[2,384]{1,0:T(2,128)S(1)} %pad_maximum_fusion.refs_0_, ...), custom_call_target="tpu_custom_call" | custom-call | flops 1000000 | tf_op jit(solution)/shard_map/pallas_call | solution.py:29
  44.0 3.6 %collective-permute-start.14 = (f32[32,384]{1,0:T(8,128)S(1)}, f32[32,384]{1,0:T(8,128)S(1)}, u32[]{:S(2)}, u32[]{:S(2)}) collective-permute-start(f32[32,384]{1,0:T(8,128)S(1)} %get-tuple-element.81), channel_id=1, source_target_pairs={{0,24},{8,0},{16,8},{24,16},{1,25},{9,1},{17,9},{25,17},{2,26},{10... | collective-permute-start | bytes 147464 | tf_op jit(solution)/shard_map/ppermute | solution.py:472
  48.8 3.2 %collective-permute-start.17 = (f32[32,384]{1,0:T(8,128)S(1)}, f32[32,384]{1,0:T(8,128)S(1)}, u32[]{:S(2)}, u32[]{:S(2)}) collective-permute-start(f32[32,384]{1,0:T(8,128)S(1)} %get-tuple-element.87), channel_id=1, source_target_pairs={{0,24},{8,0},{16,8},{24,16},{1,25},{9,1},{17,9},{25,17},{2,26},{10... | collective-permute-start | bytes 147464 | tf_op jit(solution)/shard_map/ppermute | solution.py:472
  54.0 2.6 %shard_map.85 = (f32[48,384]{1,0:T(8,128)S(1)}, f32[32,64]{1,0:T(8,128)S(1)}) custom-call(f32[6,384,384]{2,1,0:T(8,128)S(1)} %get-tuple-element.67.maps, f32[384,128]{1,0:T(8,128)S(1)} %get-tuple-element.79.sums, bf16[384,144]{1,0:T(8,128)(2,1)S(1)} %get-tuple-element.65.hot, bf16[384,64]{1,0:T(8,128)(2,1)S(1)} %get-tuple-element.80.plus, ...), custom_call_target="tpu_custom_call" | custom-call | flops 1000000 | tf_op jit(solution)/shard_map/pallas_call | solution.py:29
  59.0 1.8 %shard_map.87 = (f32[32,64]{1,0:T(8,128)S(1)}, f32[2,16,384]{2,1,0:T(8,128)S(1)}) custom-call(f32[6,384,384]{2,1,0:T(8,128)S(1)} %get-tuple-element.67.maps, f32[384,128]{1,0:T(8,128)S(1)} %shard_map.84.sums, bf16[384,144]{1,0:T(8,128)(2,1)S(1)} %get-tuple-element.65.hot, bf16[384,64]{1,0:T(8,128)(2,1)S(1)} %get-tuple-element.78.minus, ...), custom_call_target="tpu_custom_call" | custom-call | flops 1000000 | tf_op jit(solution)/shard_map/pallas_call | solution.py:29
  66.1 2.4 %collective-permute-done.22.refs_3_ = f32[32,64]{1,0:T(8,128)S(1)} collective-permute-done((f32[32,64]{1,0:T(8,128)S(1)}, f32[32,64]{1,0:T(8,128)S(1)}, u32[]{:S(2)}, u32[]{:S(2)}) %collective-permute-start.22) | collective-permute-done | bytes 8224 | tf_op jit(solution)/shard_map/ppermute | solution.py:483
  70.4 2.0 %collective-permute-start.25 = (f32[32,64]{1,0:T(8,128)S(1)}, f32[32,64]{1,0:T(8,128)S(1)}, u32[]{:S(2)}, u32[]{:S(2)}) collective-permute-start(f32[32,64]{1,0:T(8,128)S(1)} %shard_map.89.refs_0_), channel_id=1, source_target_pairs={{0,16},{8,24},{16,0},{24,8},{1,17},{9,25},{17,1},{25,9},{2,18},{10... | collective-permute-start | bytes 24584 | tf_op jit(solution)/shard_map/ppermute | solution.py:472
  73.6 1.7 %collective-permute-done.24.refs_1_ = f32[32,64]{1,0:T(8,128)S(1)} collective-permute-done((f32[32,64]{1,0:T(8,128)S(1)}, f32[32,64]{1,0:T(8,128)S(1)}, u32[]{:S(2)}, u32[]{:S(2)}) %collective-permute-start.24) | collective-permute-done | bytes 8224 | tf_op jit(solution)/shard_map/ppermute | solution.py:472
  76.1 2.1 %shard_map.90 = (f32[16,384]{1,0:T(8,128)S(1)}, f32[16,384]{1,0:T(8,128)S(1)}, f32[16,384]{1,0:T(8,128)S(1)}, f32[8,64]{1,0:T(8,128)S(1)}) custom-call(f32[6,384,384]{2,1,0:T(8,128)S(1)} %get-tuple-element.67.maps, bf16[384,144]{1,0:T(8,128)(2,1)S(1)} %get-tuple-element.65.hot, bf16[384,64]{1,0:T(8,128)(2,1)S(1)} %get-tuple-element.78.minus, ...), custom_call_target="tpu_custom_call" | custom-call | flops 1000000 | tf_op jit(solution)/shard_map/pallas_call | solution.py:29
  78.2 1.8 %collective-permute-start.27 = (f32[16,384]{1,0:T(8,128)S(1)}, f32[16,384]{1,0:T(8,128)S(1)}, u32[]{:S(2)}, u32[]{:S(2)}) collective-permute-start(f32[16,384]{1,0:T(8,128)S(1)} %get-tuple-element.93), channel_id=1, source_target_pairs={{0,8},{8,16},{16,24},{24,0},{1,9},{9,17},{17,25},{25,1},{2,10},{10... | collective-permute-start | bytes 73736 | tf_op jit(solution)/shard_map/ppermute | solution.py:472
  80.1 2.1 %collective-permute-start.28 = (f32[16,384]{1,0:T(8,128)S(1)}, f32[16,384]{1,0:T(8,128)S(1)}, u32[]{:S(2)}, u32[]{:S(2)}) collective-permute-start(f32[16,384]{1,0:T(8,128)S(1)} %get-tuple-element.94), channel_id=1, source_target_pairs={{0,24},{8,0},{16,8},{24,16},{1,25},{9,1},{17,9},{25,17},{2,26},{10... | collective-permute-start | bytes 73736 | tf_op jit(solution)/shard_map/ppermute | solution.py:472
  82.1 1.9 %collective-permute-done.27.from_prev = f32[16,384]{1,0:T(8,128)S(1)} collective-permute-done((f32[16,384]{1,0:T(8,128)S(1)}, f32[16,384]{1,0:T(8,128)S(1)}, u32[]{:S(2)}, u32[]{:S(2)}) %collective-permute-start.27) | collective-permute-done | bytes 24608 | tf_op jit(solution)/shard_map/ppermute | solution.py:472
  87.1 2.4 %collective-permute-start.32 = (f32[2,768]{1,0:T(2,128)S(1)}, f32[2,768]{1,0:T(2,128)S(1)}, u32[]{:S(2)}, u32[]{:S(2)}) collective-permute-start(f32[2,768]{1,0:T(2,128)S(1)} %get-tuple-element.100), channel_id=1, source_target_pairs={{0,6},{1,7},{2,4},{3,5},{4,2},{5,3},{6,0},{7,1},{8,14},{9,15},{10,... | collective-permute-start | bytes 18440 | tf_op jit(solution)/shard_map/ppermute | solution.py:483
  (96 shorter events, 29.6 us)
Async XLA Ops:
  2.7 15.6 %collective-permute-start.4 = (f32[2,48,768]{2,1,0:T(8,128)S(1)}, f32[2,48,768]{2,1,0:T(8,128)S(1)}, u32[]{:S(2)}, u32[]{:S(2)}) collective-permute-start(f32[2,48,768]{2,1,0:T(8,128)S(1)} %get-tuple-element.60), channel_id=1, source_target_pairs={{0,2},{1,3},{2,0},{3,1},{4,6},{5,7},{6,4},{7,5},{8,10},{9,11},{10,... | collective-permute-start | bytes 884744 | tf_op jit(solution)/shard_map/ppermute | solution.py:483
  5.7 12.6 %collective-permute-start.5 = (f32[2,48,768]{2,1,0:T(8,128)S(1)}, f32[2,48,768]{2,1,0:T(8,128)S(1)}, u32[]{:S(2)}, u32[]{:S(2)}) collective-permute-start(f32[2,48,768]{2,1,0:T(8,128)S(1)} %get-tuple-element.61), channel_id=1, source_target_pairs={{0,4},{1,5},{2,6},{3,7},{4,0},{5,1},{6,2},{7,3},{8,12},{9,13},{10,... | collective-permute-start | bytes 884744 | tf_op jit(solution)/shard_map/ppermute | solution.py:483
  8.2 5.3 %collective-permute-start = (f32[1,8,768]{2,1,0:T(8,128)S(1)}, f32[1,8,768]{2,1,0:T(8,128)S(1)}, u32[]{:S(2)}, u32[]{:S(2)}) collective-permute-start(f32[1,8,768]{2,1,0:T(8,128)S(1)} %get-tuple-element.53), channel_id=1, source_target_pairs={{0,2},{1,3},{2,0},{3,1},{4,6},{5,7},{6,4},{7,5},{8,10},{9,11},{10,... | collective-permute-start | bytes 73736 | tf_op jit(solution)/shard_map/ppermute | solution.py:483
  8.8 7.4 %collective-permute-start.1 = (f32[1,8,768]{2,1,0:T(8,128)S(1)}, f32[1,8,768]{2,1,0:T(8,128)S(1)}, u32[]{:S(2)}, u32[]{:S(2)}) collective-permute-start(f32[1,8,768]{2,1,0:T(8,128)S(1)} %get-tuple-element.54), channel_id=1, source_target_pairs={{0,4},{1,5},{2,6},{3,7},{4,0},{5,1},{6,2},{7,3},{8,12},{9,13},{10,... | collective-permute-start | bytes 73736 | tf_op jit(solution)/shard_map/ppermute | solution.py:483
  8.8 7.4 %collective-permute-start.2 = (f32[1,8,768]{2,1,0:T(8,128)S(1)}, f32[1,8,768]{2,1,0:T(8,128)S(1)}, u32[]{:S(2)}, u32[]{:S(2)}) collective-permute-start(f32[1,8,768]{2,1,0:T(8,128)S(1)} %get-tuple-element.55), channel_id=1, source_target_pairs={{0,6},{1,7},{2,4},{3,5},{4,2},{5,3},{6,0},{7,1},{8,14},{9,15},{10,... | collective-permute-start | bytes 73736 | tf_op jit(solution)/shard_map/ppermute | solution.py:483
  13.5 8.8 %collective-permute-start.6 = (f32[2,48,768]{2,1,0:T(8,128)S(1)}, f32[2,48,768]{2,1,0:T(8,128)S(1)}, u32[]{:S(2)}, u32[]{:S(2)}) collective-permute-start(f32[2,48,768]{2,1,0:T(8,128)S(1)} %get-tuple-element.62), channel_id=1, source_target_pairs={{0,6},{1,7},{2,4},{3,5},{4,2},{5,3},{6,0},{7,1},{8,14},{9,15},{10,... | collective-permute-start | bytes 884744 | tf_op jit(solution)/shard_map/ppermute | solution.py:483
  22.4 14.3 %collective-permute-start.7 = (f32[2,192,384]{2,1,0:T(8,128)S(1)}, f32[2,192,384]{2,1,0:T(8,128)S(1)}, u32[]{:S(2)}, u32[]{:S(2)}) collective-permute-start(f32[2,192,384]{2,1,0:T(8,128)S(1)} %get-tuple-element.64), channel_id=1, source_target_pairs={{0,1},{1,0},{2,3},{3,2},{4,5},{5,4},{6,7},{7,6},{8,9},{9,8},{10,11... | collective-permute-start | bytes 1769480 | tf_op jit(solution)/shard_map/ppermute | solution.py:488
  23.1 20.7 %collective-permute-start.10 = (f32[2,48,768]{2,1,0:T(8,128)S(1)}, f32[2,48,768]{2,1,0:T(8,128)S(1)}, u32[]{:S(2)}, u32[]{:S(2)}) collective-permute-start(f32[2,48,768]{2,1,0:T(8,128)S(1)} %get-tuple-element.73), channel_id=1, source_target_pairs={{0,2},{1,3},{2,0},{3,1},{4,6},{5,7},{6,4},{7,5},{8,10},{9,11},{10,... | collective-permute-start | bytes 884744 | tf_op jit(solution)/shard_map/ppermute | solution.py:483
  24.6 19.2 %collective-permute-start.11 = (f32[2,48,768]{2,1,0:T(8,128)S(1)}, f32[2,48,768]{2,1,0:T(8,128)S(1)}, u32[]{:S(2)}, u32[]{:S(2)}) collective-permute-start(f32[2,48,768]{2,1,0:T(8,128)S(1)} %get-tuple-element.74), channel_id=1, source_target_pairs={{0,4},{1,5},{2,6},{3,7},{4,0},{5,1},{6,2},{7,3},{8,12},{9,13},{10,... | collective-permute-start | bytes 884744 | tf_op jit(solution)/shard_map/ppermute | solution.py:483
  26.2 17.7 %collective-permute-start.12 = (f32[2,48,768]{2,1,0:T(8,128)S(1)}, f32[2,48,768]{2,1,0:T(8,128)S(1)}, u32[]{:S(2)}, u32[]{:S(2)}) collective-permute-start(f32[2,48,768]{2,1,0:T(8,128)S(1)} %get-tuple-element.75), channel_id=1, source_target_pairs={{0,6},{1,7},{2,4},{3,5},{4,2},{5,3},{6,0},{7,1},{8,14},{9,15},{10,... | collective-permute-start | bytes 884744 | tf_op jit(solution)/shard_map/ppermute | solution.py:483
  26.7 5.9 %collective-permute-start.8 = (f32[2,16,384]{2,1,0:T(8,128)S(1)}, f32[2,16,384]{2,1,0:T(8,128)S(1)}, u32[]{:S(2)}, u32[]{:S(2)}) collective-permute-start(f32[2,16,384]{2,1,0:T(8,128)S(1)} %get-tuple-element.58.own.table), channel_id=1, source_target_pairs={{0,8},{8,16},{16,24},{24,0},{1,9},{9,17},{17,25},{25,1},{2,10},{10... | collective-permute-start | bytes 147464 | tf_op jit(solution)/shard_map/ppermute | solution.py:472
  43.9 4.3 %collective-permute-start.13 = (f32[2,192,384]{2,1,0:T(8,128)S(1)}, f32[2,192,384]{2,1,0:T(8,128)S(1)}, u32[]{:S(2)}, u32[]{:S(2)}) collective-permute-start(f32[2,192,384]{2,1,0:T(8,128)S(1)} %get-tuple-element.77), channel_id=1, source_target_pairs={{0,1},{1,0},{2,3},{3,2},{4,5},{5,4},{6,7},{7,6},{8,9},{9,8},{10,11... | collective-permute-start | bytes 1769480 | tf_op jit(solution)/shard_map/ppermute | solution.py:488
  44.0 9.1 %collective-permute-start.14 = (f32[32,384]{1,0:T(8,128)S(1)}, f32[32,384]{1,0:T(8,128)S(1)}, u32[]{:S(2)}, u32[]{:S(2)}) collective-permute-start(f32[32,384]{1,0:T(8,128)S(1)} %get-tuple-element.81), channel_id=1, source_target_pairs={{0,24},{8,0},{16,8},{24,16},{1,25},{9,1},{17,9},{25,17},{2,26},{10... | collective-permute-start | bytes 147464 | tf_op jit(solution)/shard_map/ppermute | solution.py:472
  47.6 5.8 %collective-permute-start.15 = (f32[32,384]{1,0:T(8,128)S(1)}, f32[32,384]{1,0:T(8,128)S(1)}, u32[]{:S(2)}, u32[]{:S(2)}) collective-permute-start(f32[32,384]{1,0:T(8,128)S(1)} %get-tuple-element.82), channel_id=1, source_target_pairs={{0,16},{8,24},{16,0},{24,8},{1,17},{9,25},{17,1},{25,9},{2,18},{10... | collective-permute-start | bytes 147464 | tf_op jit(solution)/shard_map/ppermute | solution.py:472
  47.6 6.4 %collective-permute-start.16 = (f32[32,384]{1,0:T(8,128)S(1)}, f32[32,384]{1,0:T(8,128)S(1)}, u32[]{:S(2)}, u32[]{:S(2)}) collective-permute-start(f32[32,384]{1,0:T(8,128)S(1)} %get-tuple-element.83), channel_id=1, source_target_pairs={{0,8},{8,16},{16,24},{24,0},{1,9},{9,17},{17,25},{25,1},{2,10},{10... | collective-permute-start | bytes 147464 | tf_op jit(solution)/shard_map/ppermute | solution.py:472
  48.8 9.3 %collective-permute-start.17 = (f32[32,384]{1,0:T(8,128)S(1)}, f32[32,384]{1,0:T(8,128)S(1)}, u32[]{:S(2)}, u32[]{:S(2)}) collective-permute-start(f32[32,384]{1,0:T(8,128)S(1)} %get-tuple-element.87), channel_id=1, source_target_pairs={{0,24},{8,0},{16,8},{24,16},{1,25},{9,1},{17,9},{25,17},{2,26},{10... | collective-permute-start | bytes 147464 | tf_op jit(solution)/shard_map/ppermute | solution.py:472
  52.0 6.1 %collective-permute-start.18 = (f32[32,384]{1,0:T(8,128)S(1)}, f32[32,384]{1,0:T(8,128)S(1)}, u32[]{:S(2)}, u32[]{:S(2)}) collective-permute-start(f32[32,384]{1,0:T(8,128)S(1)} %get-tuple-element.88), channel_id=1, source_target_pairs={{0,16},{8,24},{16,0},{24,8},{1,17},{9,25},{17,1},{25,9},{2,18},{10... | collective-permute-start | bytes 147464 | tf_op jit(solution)/shard_map/ppermute | solution.py:472
  53.1 5.9 %collective-permute-start.19 = (f32[32,384]{1,0:T(8,128)S(1)}, f32[32,384]{1,0:T(8,128)S(1)}, u32[]{:S(2)}, u32[]{:S(2)}) collective-permute-start(f32[32,384]{1,0:T(8,128)S(1)} %get-tuple-element.89), channel_id=1, source_target_pairs={{0,8},{8,16},{16,24},{24,0},{1,9},{9,17},{17,25},{25,1},{2,10},{10... | collective-permute-start | bytes 147464 | tf_op jit(solution)/shard_map/ppermute | solution.py:472
  63.9 4.6 %collective-permute-start.22 = (f32[32,64]{1,0:T(8,128)S(1)}, f32[32,64]{1,0:T(8,128)S(1)}, u32[]{:S(2)}, u32[]{:S(2)}) collective-permute-start(f32[32,64]{1,0:T(8,128)S(1)} %get-tuple-element.91.refs_0_), channel_id=1, source_target_pairs={{0,6},{1,7},{2,4},{3,5},{4,2},{5,3},{6,0},{7,1},{8,14},{9,15},{10,... | collective-permute-start | bytes 24584 | tf_op jit(solution)/shard_map/ppermute | solution.py:483
  69.8 5.5 %collective-permute-start.24 = (f32[32,64]{1,0:T(8,128)S(1)}, f32[32,64]{1,0:T(8,128)S(1)}, u32[]{:S(2)}, u32[]{:S(2)}) collective-permute-start(f32[32,64]{1,0:T(8,128)S(1)} %shard_map.89.refs_0_), channel_id=1, source_target_pairs={{0,8},{8,16},{16,24},{24,0},{1,9},{9,17},{17,25},{25,1},{2,10},{10... | collective-permute-start | bytes 24584 | tf_op jit(solution)/shard_map/ppermute | solution.py:472
  70.4 4.9 %collective-permute-start.25 = (f32[32,64]{1,0:T(8,128)S(1)}, f32[32,64]{1,0:T(8,128)S(1)}, u32[]{:S(2)}, u32[]{:S(2)}) collective-permute-start(f32[32,64]{1,0:T(8,128)S(1)} %shard_map.89.refs_0_), channel_id=1, source_target_pairs={{0,16},{8,24},{16,0},{24,8},{1,17},{9,25},{17,1},{25,9},{2,18},{10... | collective-permute-start | bytes 24584 | tf_op jit(solution)/shard_map/ppermute | solution.py:472
  78.2 5.8 %collective-permute-start.27 = (f32[16,384]{1,0:T(8,128)S(1)}, f32[16,384]{1,0:T(8,128)S(1)}, u32[]{:S(2)}, u32[]{:S(2)}) collective-permute-start(f32[16,384]{1,0:T(8,128)S(1)} %get-tuple-element.93), channel_id=1, source_target_pairs={{0,8},{8,16},{16,24},{24,0},{1,9},{9,17},{17,25},{25,1},{2,10},{10... | collective-permute-start | bytes 73736 | tf_op jit(solution)/shard_map/ppermute | solution.py:472
  86.0 4.3 %collective-permute-start.30 = (f32[2,768]{1,0:T(2,128)S(1)}, f32[2,768]{1,0:T(2,128)S(1)}, u32[]{:S(2)}, u32[]{:S(2)}) collective-permute-start(f32[2,768]{1,0:T(2,128)S(1)} %get-tuple-element.98), channel_id=1, source_target_pairs={{0,2},{1,3},{2,0},{3,1},{4,6},{5,7},{6,4},{7,5},{8,10},{9,11},{10,... | collective-permute-start | bytes 18440 | tf_op jit(solution)/shard_map/ppermute | solution.py:483
  87.1 4.5 %collective-permute-start.32 = (f32[2,768]{1,0:T(2,128)S(1)}, f32[2,768]{1,0:T(2,128)S(1)}, u32[]{:S(2)}, u32[]{:S(2)}) collective-permute-start(f32[2,768]{1,0:T(2,128)S(1)} %get-tuple-element.100), channel_id=1, source_target_pairs={{0,6},{1,7},{2,4},{3,5},{4,2},{5,3},{6,0},{7,1},{8,14},{9,15},{10,... | collective-permute-start | bytes 18440 | tf_op jit(solution)/shard_map/ppermute | solution.py:483
  (15 other events, 75.5 us)
